TPU v7x, 256 devices: a whole 4x4x8 slice. The times are simulated.
256 devices in a mesh: blk: 32 (over z, y), lblk: 8 (over x, core).
Axes of the slice: x: 4, y: 4, z: 8, core: 2. Of those that a mesh axis runs over, the one named last changes fastest.
Arguments:
- partial_rows: bfloat16 [8, 32768, 1024], P('lblk', 'blk'), may hold values from -5 to 5
- row_owner: int32 [8, 32768, 1], P('lblk', 'blk'), may hold values from 0 to 31; in each aligned block of 1024 rows (0 to 1023, 1024 to 2047, ..., all dimensions but the last counted through in order) at most 128 rows name the same one
- row_key: int32 [8, 32768], P('lblk', 'blk'), may hold values from 0 to 127
- azimuth_orders: int32 [32], replicated, may hold values from 1 to 4095, as said below
- legendre_table: bfloat16 [32, 4096, 2048], P('blk', 'lblk'), may hold values from -0.125 to 0.125
- spin_even: bfloat16 [32, 4096, 2048], P('blk', 'lblk'), may hold values from -0.125 to 0.125
- spin_odd: bfloat16 [32, 4096, 2048], P('blk', 'lblk'), may hold values from -0.125 to 0.125
Outputs:
- eigenvalues: float32 [2, 2, 8, 256, 8192], P(None, None, 'lblk', 'blk')
- cycle_maps: float32 [2, 8, 256, 8192], P(None, 'lblk', 'blk')
Inputs may be any that keep to these rules, and one draw needn't show every extreme that they name: `row_owner`: no more than 128 rows of one device name the same owner; some device sends exactly 128 rows to some owner in every draw. `azimuth_orders`: all distinct; 1 and 4095 are always among them.
All inputs are finite; a program needn't handle non-finite values.
Results may differ from a plain program's by a relative error of at most 0.0041.
Values may be sent and summed in bfloat16 or wider, within the bound.
No kernel may reach another device: no remote copies, remote signals or barrier semaphores. Data moves between devices by JAX's collectives and lax.ppermute only.
A program may use at most 128 MiB of HBM per device.

v0:
```python
import functools
import math

import jax
import jax.numpy as jnp
from jax import lax
from jax.experimental import pallas as pl
from jax.experimental.pallas import tpu as pltpu
from jax.sharding import Mesh
from jax.sharding import PartitionSpec as P


NPHI = 8192
L = 4096
SEG = 1024
R_DEV = 8
PR = 1024
KEYS = 128
POS = NPHI // SEG
BLK = ("blk_0", "blk_1")

NT = (((1,), (1,)), ((), ()))
NN = (((1,), (0,)), ((), ()))


def halves(x):
    high = x.astype(jnp.bfloat16)
    low = (x - high.astype(jnp.float32)).astype(jnp.bfloat16)
    return high, low


def dot32(a, b, dims):
    return lax.dot_general(a, b, dims, preferred_element_type=jnp.float32)


def wave_tables(azimuth_orders):
    orders = azimuth_orders.shape[0]
    trig = lax.broadcasted_iota(jnp.int32, (2, orders, SEG), 0)
    pixel = lax.broadcasted_iota(jnp.int32, (2, orders, SEG), 2)
    phase = pixel * azimuth_orders[None, :, None] - trig * (NPHI // 4)
    angles = (phase & (NPHI - 1)).astype(jnp.float32) * (2.0 * math.pi / NPHI)
    return jnp.cos(angles).reshape(2 * orders, SEG)


def eighth_turn(index):
    angle = (index & (POS - 1)).astype(jnp.float32) * (2.0 * math.pi / POS)
    return jnp.cos(angle), jnp.sin(angle)


def modes_kernel(slices, rows_ref, owner_ref, key_ref, wave_ref, out_ref):
    orders = wave_ref.shape[0] // 2
    w_high, w_low = halves(wave_ref[...])
    rows = rows_ref[...]
    seg = dot32(w_high, rows, NT) + dot32(w_low, rows, NT)
    cos_part, sin_part = seg[:orders], seg[orders:]
    key = key_ref[...]
    half = wave_ref[:, SEG // 2 : SEG // 2 + 1]
    turn_cos, turn_sin = half[:orders], half[orders:]
    for bit in range(3):
        turn_cos, turn_sin = turn_cos * turn_cos - turn_sin * turn_sin, 2.0 * turn_cos * turn_sin
        turned = (key & (1 << bit)) != 0
        step_cos = jnp.where(turned, turn_cos, 1.0)
        step_sin = jnp.where(turned, turn_sin, 0.0)
        cos_part, sin_part = (
            cos_part * step_cos - sin_part * step_sin,
            sin_part * step_cos + cos_part * step_sin,
        )
    modes = jnp.concatenate([cos_part, sin_part], axis=0)
    cycles = slices * R_DEV
    slot = (key >> 6) * cycles + owner_ref[...] * R_DEV + ((key >> 3) & (R_DEV - 1))
    pick = lax.broadcasted_iota(jnp.int32, (2 * cycles, PR), 0) == slot
    pick = jnp.where(pick, 1.0, 0.0).astype(jnp.bfloat16)
    m_high, m_low = halves(modes)
    sums = dot32(m_high, pick, NT) + dot32(m_low, pick, NT)
    parts = cycles // 128
    for trig in range(2):
        for shell in range(2):
            for part in range(parts):
                out_ref[:, part * 4 + trig * 2 + shell, :] = sums[
                    trig * orders : (trig + 1) * orders,
                    shell * cycles + part * 128 : shell * cycles + (part + 1) * 128,
                ]


def local_modes(rows, owners, keys, waves, groups):
    orders = waves.shape[0] // 2
    return pl.pallas_call(
        functools.partial(modes_kernel, groups),
        out_shape=jax.ShapeDtypeStruct((orders, groups * R_DEV * 4 // 128, 128), jnp.float32),
        name="modes",
    )(rows, owners, keys, waves)


def harmonics_kernel(in_ref, out_ref):
    total = jnp.sum(in_ref[...], axis=0) * (1.0 / math.sqrt(NPHI))
    row = lax.broadcasted_iota(jnp.int32, total.shape, 0)
    total = jnp.where((row & 2) == 0, total, -total)
    out_ref[...] = jnp.broadcast_to(total[None], out_ref.shape).astype(out_ref.dtype)


def harmonics_for_all(arrived, copies):
    return pl.pallas_call(
        harmonics_kernel,
        out_shape=jax.ShapeDtypeStruct((copies, *arrived.shape[1:]), jnp.bfloat16),
        in_specs=[pl.BlockSpec(memory_space=pltpu.VMEM)],
        name="harmonics",
    )(in_vmem(arrived))


def legendre_kernel(first_ref, modes_ref, leg_ref, even_hbm, odd_hbm, out_ref, even, odd, sem):
    even_copy = pltpu.make_async_copy(even_hbm, even, sem.at[0])
    odd_copy = pltpu.make_async_copy(odd_hbm, odd, sem.at[1])
    even_copy.start()
    odd_copy.start()
    blocks, rows = modes_ref.shape[0], modes_ref.shape[1]
    pieces = []
    for block in range(blocks):
        value = modes_ref[block].astype(jnp.float32)
        for part in range(rows // 4):
            pieces.append(value[part * 4 : (part + 1) * 4])
    spectrum = jnp.concatenate(pieces, axis=1).astype(jnp.bfloat16)
    coefficients = dot32(spectrum, leg_ref[0], NT)
    width = coefficients.shape[1]
    degree = first_ref[0] + lax.broadcasted_iota(jnp.int32, (1, width), 1)
    degree = degree.astype(jnp.float32)
    smoothing = jnp.exp(-2.0 * degree * (degree + 1.0) / (L * L))
    factor = jnp.sqrt(
        jnp.maximum((degree - 1.0) * (degree + 2.0), 0.0)
        / jnp.maximum(degree * (degree + 1.0), 1.0)
    )
    trace_terms = (smoothing * coefficients).astype(jnp.bfloat16)
    shear_terms = ((-0.5 * smoothing * factor) * coefficients).astype(jnp.bfloat16)
    own = out_ref.shape[2]

    def put(kind, value):
        for block in range(blocks):
            out_ref[block, kind * 4 : kind * 4 + 4, :] = value[:, block * own : (block + 1) * own]

    put(0, dot32(trace_terms, leg_ref[0], NN))
    even_copy.wait()
    put(1, dot32(shear_terms, even[0], NN))
    odd_copy.wait()
    put(2, dot32(shear_terms, odd[0], NN))


def legendre_pair(first_degree, modes, legendre_table, spin_even, spin_odd):
    vmem = pl.BlockSpec(memory_space=pltpu.VMEM)
    left = pl.BlockSpec(memory_space=pl.ANY)
    blocks = modes.shape[0]
    cycles = legendre_table.shape[2]
    return pl.pallas_call(
        legendre_kernel,
        out_shape=jax.ShapeDtypeStruct((blocks, 12, cycles // blocks), jnp.float32),
        in_specs=[pl.BlockSpec(memory_space=pltpu.SMEM), vmem, vmem, left, left],
        out_specs=vmem,
        scratch_shapes=[
            pltpu.VMEM(spin_even.shape, spin_even.dtype),
            pltpu.VMEM(spin_odd.shape, spin_odd.dtype),
            pltpu.SemaphoreType.DMA((2,)),
        ],
        name="legendre",
    )(first_degree, in_vmem(modes), legendre_table, spin_even, spin_odd)


def fields_kernel(scale, terms_ref, order_ref, wave_ref, out_ref):
    position = pl.program_id(0)
    turn_cos, turn_sin = eighth_turn(order_ref[...] * position)
    real, imag = [], []
    for kind in range(3):
        for shell in range(2):
            cos_term, sin_term = terms_ref[kind * 4 + shell], terms_ref[kind * 4 + 2 + shell]
            real.append(-sin_term if kind == 2 else cos_term)
            imag.append(cos_term if kind == 2 else sin_term)
    real = jnp.concatenate(real, axis=0)
    imag = jnp.concatenate(imag, axis=0)
    turned = jnp.concatenate(
        [real * turn_cos - imag * turn_sin, -(real * turn_sin + imag * turn_cos)], axis=1
    )
    t_high, t_low = halves(turned)
    w_high, w_low = halves(wave_ref[...])
    fields = (dot32(t_high, w_high, NN) + (dot32(t_high, w_low, NN) + dot32(t_low, w_high, NN))) * scale
    fields = fields.reshape(3, 2, R_DEV, SEG)
    for shell in range(2):
        half_trace = 0.5 * fields[0, shell]
        first, second = fields[1, shell], fields[2, shell]
        size = jnp.sqrt(first * first + second * second)
        out_ref[0, shell, 0] = half_trace + size
        out_ref[1, shell, 0] = half_trace - size


def eigenvalues(terms, azimuth_orders, waves):
    orders = azimuth_orders.shape[0]
    whole = lambda *shape: pl.BlockSpec(shape, lambda p: (0,) * len(shape))
    return pl.pallas_call(
        functools.partial(fields_kernel, 2.0 / math.sqrt(orders)),
        out_shape=jax.ShapeDtypeStruct((2, 2, 1, R_DEV, NPHI), jnp.float32),
        grid=(POS,),
        in_specs=[whole(12, R_DEV, orders), whole(1, orders), whole(2 * orders, SEG)],
        out_specs=pl.BlockSpec((2, 2, 1, R_DEV, SEG), lambda p: (0, 0, 0, 0, p)),
        name="fields",
    )(terms, azimuth_orders[None], waves)


def shifted(x, axis, by):
    size = lax.axis_size(axis)
    return lax.ppermute(x, axis, [(i, (i + by) % size) for i in range(size)])


def add_kernel(*refs):
    moving, own_hbm, out_hbm = refs[:2], refs[2:4], refs[4:6]
    own, result, sems = refs[6:8], refs[8:10], refs[10]
    size, whole = moving[0].shape[0], own[0].shape[0]
    copies = []
    for side in range(2):
        copies.append(pltpu.make_async_copy(own_hbm[side], own[side], sems.at[side]))
        copies[-1].start()
    sent = []
    for side, lead in ((0, 0), (1, whole - size)):
        copies[side].wait()
        if size < whole:
            other = size - lead
            kept = own[side][other : other + size]
            result[side][other : other + size] = kept.astype(result[side].dtype)
        added = own[side][lead : lead + size] + moving[side][...].astype(jnp.float32)
        result[side][lead : lead + size] = added.astype(result[side].dtype)
        sent.append(pltpu.make_async_copy(result[side], out_hbm[side], sems.at[2 + side]))
        sent[-1].start()
    for copy in sent:
        copy.wait()


def in_vmem(x):
    return pltpu.with_memory_space_constraint(x, pltpu.VMEM)


def ring_add(up, down, up_own, down_own):
    vmem = pl.BlockSpec(memory_space=pltpu.VMEM)
    hbm = pl.BlockSpec(memory_space=pltpu.HBM)
    result = jax.ShapeDtypeStruct(up_own.shape, up.dtype)
    return pl.pallas_call(
        add_kernel,
        out_shape=(result, result),
        in_specs=[vmem, vmem, hbm, hbm],
        out_specs=(hbm, hbm),
        scratch_shapes=[pltpu.VMEM(up_own.shape, up_own.dtype)] * 2
        + [pltpu.VMEM(up_own.shape, up.dtype)] * 2
        + [pltpu.SemaphoreType.DMA((4,))],
        name="ring_add",
    )(in_vmem(up), in_vmem(down), up_own, down_own)


def ring_sums(chunks, far, axis, token):
    size = len(chunks)
    middle = size // 2
    up, down = far
    for distance in range(middle - 1, -1, -1):
        up = shifted(up, axis, 1)
        down = shifted(down, axis, -1)
        if distance > 0:
            own = chunks[distance]
            if distance == middle - 1:
                own = after(own, token)
            up, down = ring_add(up, down, own, chunks[size - distance])
    return chunks[0], up, down


def after(x, token):
    return lax.optimization_barrier((x, token))[0]


DIGIT = 64
TILE = 256
EXTRA = 16


def pack_kernel(rows_ref, owner_ref, key_ref, *outs):
    size, lanes = rows_ref.shape[0] // len(outs), rows_ref.shape[1]
    key = key_ref[...]
    place = (key & 64) + (key & 7) * R_DEV + ((key >> 3) & 7)
    slot = owner_ref[...] * KEYS + place
    row = lax.broadcasted_iota(jnp.int32, (EXTRA, size), 0)
    for part, out in enumerate(outs):
        own = slot[:, part * size : (part + 1) * size]
        tail = jnp.where(row == 0, own // DIGIT, jnp.where(row == 1, own % DIGIT, 0))
        out[:size] = rows_ref[part * size : (part + 1) * size]
        out[size:] = jnp.zeros((EXTRA, lanes), out.dtype)
        out[size:, :size] = tail.astype(jnp.float32).astype(out.dtype)


def row_pieces(rows, owners, keys, parts):
    piece = jax.ShapeDtypeStruct((rows.shape[0] // parts + EXTRA, rows.shape[1]), rows.dtype)
    return pl.pallas_call(pack_kernel, out_shape=(piece,) * parts, name="pack")(
        rows, owners[None], keys[None]
    )


def sums_kernel(count, has_base, columns, rings, place_ref, *refs):
    pieces, tails = refs[:count], refs[count : 2 * count]
    outs, pick_ref = refs[2 * count + has_base : -1], refs[-1]
    slots = pick_ref.shape[0]
    size = pieces[0].shape[0]

    @pl.when(pl.program_id(0) == 0)
    def _():
        my_z, my_y = place_ref[0], place_ref[1]
        for index, tail_ref in enumerate(tails):
            tail = tail_ref[:, :size].astype(jnp.float32).astype(jnp.int32)
            slot = tail[0:1] * DIGIT + tail[1:2]
            owner = slot // KEYS
            distance = (owner // columns - my_z) & (rings - 1)
            mine = distance * KEYS + (slot & (KEYS - 1))
            mine = jnp.where((owner & (columns - 1)) == my_y, mine, -1)
            pick = lax.broadcasted_iota(jnp.int32, (slots, size), 0) == mine
            pick_ref[:, index * size : (index + 1) * size] = jnp.where(pick, 1.0, 0.0).astype(
                jnp.bfloat16
            )

    total = refs[2 * count][...] if has_base else 0.0
    for index, piece in enumerate(pieces):
        total = total + dot32(pick_ref[:, index * size : (index + 1) * size], piece[...], NN)
    start = 0
    for out in outs:
        out[...] = total[start : start + out.shape[0]].astype(out.dtype)
        start += out.shape[0]


def sum_pieces(pieces, base, place, outs):
    columns, rings = lax.axis_size(BLK[1]), lax.axis_size(BLK[0])
    size, lanes = pieces[0].shape[0] - EXTRA, pieces[0].shape[1]
    slots = rings * KEYS
    specs = [pl.BlockSpec(memory_space=pltpu.SMEM)]
    specs += [pl.BlockSpec((size, TILE), lambda n: (0, n)) for _ in pieces]
    specs += [pl.BlockSpec((EXTRA, lanes), lambda n: (size // EXTRA, 0)) for _ in pieces]
    operands = [*pieces, *pieces]
    if base is not None:
        specs.append(pl.BlockSpec((slots, TILE), lambda n: (0, n)))
        operands.append(base)
    return pl.pallas_call(
        functools.partial(sums_kernel, len(pieces), int(base is not None), columns, rings),
        out_shape=tuple(jax.ShapeDtypeStruct((rows, lanes), dtype) for rows, dtype in outs),
        grid=(lanes // TILE,),
        in_specs=specs,
        out_specs=tuple(pl.BlockSpec((rows, TILE), lambda n: (0, n)) for rows, _ in outs),
        scratch_shapes=[pltpu.VMEM((slots, size * len(pieces)), jnp.bfloat16)],
    )(place, *operands)


class ColumnSums:
    def __init__(self, rows, owners, keys, waves):
        axis = BLK[1]
        self.place = jnp.stack([lax.axis_index(BLK[0]), lax.axis_index(BLK[1])]).astype(jnp.int32)
        self.pieces = first, last = row_pieces(rows, owners, keys, 2)
        self.up = [shifted(first, axis, 1), shifted(last, axis, 1)]
        self.down = [shifted(after(last, waves), axis, -1), shifted(first, axis, -1)]

    def forward(self, token):
        self.up_far = shifted(after(self.up[0], token), BLK[1], 1)
        self.down_far = shifted(after(self.down[0], token), BLK[1], -1)

    def finish(self, token):
        rings = lax.axis_size(BLK[0])
        whole = [(rings * KEYS, jnp.float32)]
        (sums,) = sum_pieces(self.pieces, None, self.place, whole)
        near, following = [self.up[0], self.down[0]], [self.up[1], self.down[1]]
        (sums,) = sum_pieces(near, sums, self.place, whole)
        (sums,) = sum_pieces(following, sums, self.place, whole)
        one, half = (KEYS, jnp.float32), (KEYS // 2, jnp.bfloat16)
        side = [one] * (rings // 2)
        outs = [*side, half, half, *side[1:]]
        parts = sum_pieces([self.up_far, self.down_far], sums, self.place, outs)
        middle = rings // 2
        chunks = [*parts[:middle], None, *parts[middle + 2 :]]
        return ring_sums(chunks, parts[middle : middle + 2], BLK[0], token)


def maps_kernel(own, up, down, out_ref):
    for shell in range(2):
        for position in range(POS):
            row = pl.ds((shell * POS + position) * R_DEV, R_DEV)
            total = own[row] + up[row].astype(jnp.float32) + down[row].astype(jnp.float32)
            out_ref[shell, 0, :, position * SEG : (position + 1) * SEG] = total


def map_output(own, up, down):
    vmem = pl.BlockSpec(memory_space=pltpu.VMEM)
    return pl.pallas_call(
        maps_kernel,
        out_shape=jax.ShapeDtypeStruct((2, 1, R_DEV, NPHI), jnp.float32),
        in_specs=[vmem] * 3,
        name="maps",
    )(own, in_vmem(up), in_vmem(down))


def body(partial_rows, row_owner, row_key, azimuth_orders, legendre_table, spin_even, spin_odd):
    groups = lax.axis_size(BLK)
    blocks = lax.axis_size("lblk")
    rows = partial_rows[0]
    owners = row_owner[0, :, 0]
    keys = row_key[0]
    orders = azimuth_orders.shape[0]
    waves = wave_tables(azimuth_orders)

    columns = ColumnSums(rows, owners, keys, waves)
    sums = local_modes(rows, owners[None], keys[None], waves, groups)
    arrived = lax.all_to_all(sums, BLK, split_axis=0, concat_axis=0, tiled=True)
    columns.forward(arrived)
    modes = harmonics_for_all(arrived, blocks)
    modes = lax.all_to_all(modes, "lblk", 0, 0, tiled=True)
    first_degree = (lax.axis_index("lblk") * legendre_table.shape[1]).astype(jnp.int32)[None]
    pieces = legendre_pair(first_degree, modes, legendre_table, spin_even, spin_odd)
    pieces = lax.all_to_all(pieces, "lblk", split_axis=0, concat_axis=0, tiled=True)
    summed = pieces.sum(axis=0).astype(jnp.bfloat16)
    summed = summed.reshape(12, groups, R_DEV).transpose(1, 0, 2).reshape(groups, 12 * R_DEV)
    returned = lax.all_to_all(summed, BLK, split_axis=0, concat_axis=0, tiled=True)
    terms = returned.astype(jnp.float32).T.reshape(12, R_DEV, orders)
    eigen = eigenvalues(terms, azimuth_orders, waves)
    return (eigen, map_output(*columns.finish(returned)))


def solution(mesh):
    finer = Mesh(mesh.devices.reshape(8, 4, mesh.shape["lblk"]), ("blk_0", "blk_1", "lblk"))
    placed = (
        P("lblk", BLK, None),
        P("lblk", BLK, None),
        P("lblk", BLK),
        P(),
        P(BLK, "lblk", None),
        P(BLK, "lblk", None),
        P(BLK, "lblk", None),
    )
    return jax.shard_map(
        body,
        mesh=finer,
        in_specs=placed,
        out_specs=(P(None, None, "lblk", BLK, None), P(None, "lblk", BLK, None)),
        check_vma=False,
    )
```

profile of v0, /device:TPU:8, one launch (start us, length us, event | category | flops | bytes accessed | tf_op | source)
XLA Modules:
  0.0 146.7 jit_solution(9808478326481157029)
XLA Ops:
  1.5 1.6 %multiply_cosine_fusion.wave_ref = f32[64,1024]{1,0:T(8,128)} fusion(s32[64]{0:T(128)S(1)} %iota.19, s32[64]{0:T(128)S(1)} %mul.32), kind=kLoop, calls=%fused_computation | loop fusion | flops 327680 | bytes 262656 | tf_op jit(solution)/shard_map/cos | solution.py:42
  3.2 3.1 %pack.1 = (bf16[528,1024]{1,0:T(8,128)(2,1)}, bf16[528,1024]{1,0:T(8,128)(2,1)}) custom-call(bf16[1024,1024]{1,0:T(8,128)(2,1)} %bitcast.14, s32[1,1024]{1,0:T(1,128)} %bitcast.19, s32[1,1024]{1,0:T(1,128)} %key_ref.3), custom_call_target="tpu_custom_call" | custom-call | tf_op jit(solution)/shard_map/pack/pallas_call | solution.py:292
  6.2 2.2 %collective-permute-start.2 = (bf16[528,1024]{1,0:T(8,128)(2,1)}, bf16[528,1024]{1,0:T(8,128)(2,1)S(1)}, u32[]{:S(2)}, u32[]{:S(2)}) collective-permute-start(bf16[528,1024]{1,0:T(8,128)(2,1)} %get-tuple-element.26.refs_1_.refs_3_), channel_id=1, source_target_pairs={{0,24},{8,0},{16,8},{24,16},{1,25},{9,1},{17,9},{25,17},{2,26},{10... | collective-permute-start | bytes 3244040 | tf_op jit(solution)/shard_map/ppermute | solution.py:206
  8.4 4.5 %modes.1 = f32[32,8,128]{2,1,0:T(8,128)} custom-call(bf16[1024,1024]{1,0:T(8,128)(2,1)} %bitcast.15, s32[1,1024]{1,0:T(1,128)} %bitcast.20, s32[1,1024]{1,0:T(1,128)} %key_ref.3, f32[64,1024]{1,0:T(8,128)} %multiply_cosine_fusion.wave_ref), custom_call_target="tpu_custom_call" | custom-call | tf_op jit(solution)/shard_map/modes/pallas_call | solution.py:87
  12.9 12.5 %all-to-all-start = ((f32[32,8,128]{2,1,0:T(8,128)}), f32[32,8,128]{2,1,0:T(8,128)S(1)}, u32[]{:S(2)}, u32[]{:S(2)}) async-start(f32[32,8,128]{2,1,0:T(8,128)} %modes.1), calls=%async_computation | async-start | bytes 262144 | tf_op jit(solution)/shard_map/all_to_all | solution.py:405
  25.4 1.5 %collective-permute-start.4 = (bf16[528,1024]{1,0:T(8,128)(2,1)}, bf16[528,1024]{1,0:T(8,128)(2,1)}, u32[]{:S(2)}, u32[]{:S(2)}) collective-permute-start(bf16[528,1024]{1,0:T(8,128)(2,1)} %get-tuple-element.26.refs_1_.refs_3_), channel_id=1, source_target_pairs={{0,8},{8,16},{16,24},{24,0},{1,9},{9,17},{17,25},{25,1},{2,10},{10... | collective-permute-start | bytes 3244040 | tf_op jit(solution)/shard_map/ppermute | solution.py:206
  27.5 9.1 %all-to-all-done.in_ref = f32[32,8,128]{2,1,0:T(8,128)S(1)} async-done(((f32[32,8,128]{2,1,0:T(8,128)}), f32[32,8,128]{2,1,0:T(8,128)S(1)}, u32[]{:S(2)}, u32[]{:S(2)}) %all-to-all-start) | async-done | bytes 131104 | tf_op jit(solution)/shard_map/all_to_all | solution.py:405
  36.7 2.6 %collective-permute-start.3 = (bf16[528,1024]{1,0:T(8,128)(2,1)S(1)}, bf16[528,1024]{1,0:T(8,128)(2,1)}, u32[]{:S(2)}, u32[]{:S(2)}) collective-permute-start(bf16[528,1024]{1,0:T(8,128)(2,1)S(1)} %collective-permute-done.2.refs_1_.refs_3_), channel_id=1, source_target_pairs={{0,24},{8,0},{16,8},{24,16},{1,25},{9,1},{17,9},{25,17},{2,26},{10... | collective-permute-start | bytes 3244040 | tf_op jit(solution)/shard_map/ppermute | solution.py:206
  40.0 4.3 %all-to-all-start.1 = ((bf16[8,8,128]{2,1,0:T(8,128)(2,1)}), bf16[8,8,128]{2,1,0:T(8,128)(2,1)S(1)}, u32[]{:S(2)}, u32[]{:S(2)}) async-start(bf16[8,8,128]{2,1,0:T(8,128)(2,1)} %harmonics.1), calls=%async_computation.1 | async-start | bytes 32768 | tf_op jit(solution)/shard_map/all_to_all | solution.py:408
  44.3 5.4 %all-to-all-done.1.modes_ref = bf16[8,8,128]{2,1,0:T(8,128)(2,1)S(1)} async-done(((bf16[8,8,128]{2,1,0:T(8,128)(2,1)}), bf16[8,8,128]{2,1,0:T(8,128)(2,1)S(1)}, u32[]{:S(2)}, u32[]{:S(2)}) %all-to-all-start.1) | async-done | bytes 16416 | tf_op jit(solution)/shard_map/all_to_all | solution.py:408
  49.7 5.4 %legendre.1 = f32[8,12,256]{2,1,0:T(8,128)} custom-call(s32[1]{0:T(128)} %bitcast.first_ref, bf16[8,8,128]{2,1,0:T(8,128)(2,1)S(1)} %all-to-all-done.1.modes_ref, bf16[1,512,2048]{2,1,0:T(8,128)(2,1)} %leg_ref.1, bf16[1,512,2048]{2,1,0:T(8,128)(2,1)} %even_hbm.1, bf16[1,512,2048]{2,1,0:T(8,128)(2,1)} %odd_hbm.1), custom_call_target="tpu_custom_call" | custom-call | tf_op jit(solution)/shard_map/legendre/pallas_call | solution.py:151
  55.1 3.4 %all-to-all-start.2 = ((f32[8,12,256]{2,1,0:T(8,128)}), f32[8,12,256]{2,1,0:T(8,128)S(1)}, u32[]{:S(2)}, u32[]{:S(2)}) async-start(f32[8,12,256]{2,1,0:T(8,128)} %legendre.1), calls=%async_computation.2 | async-start | bytes 262144 | tf_op jit(solution)/shard_map/all_to_all | solution.py:411
  58.5 6.0 %all-to-all-done.2 = f32[8,12,256]{2,1,0:T(8,128)S(1)} async-done(((f32[8,12,256]{2,1,0:T(8,128)}), f32[8,12,256]{2,1,0:T(8,128)S(1)}, u32[]{:S(2)}, u32[]{:S(2)}) %all-to-all-start.2) | async-done | bytes 98336 | tf_op jit(solution)/shard_map/all_to_all | solution.py:411
  65.5 11.3 %all-to-all-start.3 = ((bf16[32,1,96]{2,1,0:T(2,128)(2,1)}), bf16[32,1,96]{2,1,0:T(2,128)(2,1)S(1)}, u32[]{:S(2)}, u32[]{:S(2)}) async-start(bf16[32,1,96]{2,1,0:T(2,128)(2,1)} %copy.14), calls=%async_computation.3 | async-start | bytes 32768 | tf_op jit(solution)/shard_map/all_to_all | solution.py:414
  77.5 6.2 %shard_map.86.refs_4_ = f32[1024,1024]{1,0:T(8,128)} custom-call(s32[2]{0:T(128)} %pad_add_fusion.place_ref, bf16[528,1024]{1,0:T(8,128)(2,1)} %get-tuple-element.23.refs_0_.refs_2_, bf16[528,1024]{1,0:T(8,128)(2,1)} %get-tuple-element.26.refs_1_.refs_3_, bf16[528,1024]{1,0:T(8,128)(2,1)} %get-tuple-element.23.refs_0_.refs_2_, ...), custom_call_target="tpu_custom_call" | custom-call | tf_op jit(solution)/shard_map/pallas_call | solution.py:338
  83.6 7.2 %shard_map.87.refs_4_ = f32[1024,1024]{1,0:T(8,128)} custom-call(s32[2]{0:T(128)} %pad_add_fusion.place_ref, bf16[528,1024]{1,0:T(8,128)(2,1)} %copy-done.1, bf16[528,1024]{1,0:T(8,128)(2,1)} %copy-done, bf16[528,1024]{1,0:T(8,128)(2,1)} %copy-done.1, bf16[528,1024]{1,0:T(8,128)(2,1)} %copy-done, f32[1024,1024]{1,0:T(8,128)} %shard_map.86.refs_4_), custom_call_target="tpu_custom_call" | custom-call | tf_op jit(solution)/shard_map/pallas_call | solution.py:338
  90.8 7.1 %shard_map.88.refs_4_ = f32[1024,1024]{1,0:T(8,128)} custom-call(s32[2]{0:T(128)} %pad_add_fusion.place_ref, bf16[528,1024]{1,0:T(8,128)(2,1)} %collective-permute-done.4.refs_0_.refs_2_, bf16[528,1024]{1,0:T(8,128)(2,1)} %collective-permute-done.5.refs_1_.refs_3_, bf16[528,1024]{1,0:T(8,128)(2,1)} %collective-permute-done.4.refs_0_.refs_2_, ...), custom_call_target="tpu_custom_call" | custom-call | tf_op jit(solution)/shard_map/pallas_call | solution.py:338
  97.9 6.6 %shard_map.89 = (f32[128,1024]{1,0:T(8,128)}, f32[128,1024]{1,0:T(8,128)}, f32[128,1024]{1,0:T(8,128)}, f32[128,1024]{1,0:T(8,128)}, bf16[64,1024]{1,0:T(8,128)(...) custom-call(s32[2]{0:T(128)} %pad_add_fusion.place_ref, ...), custom_call_target="tpu_custom_call" | custom-call | tf_op jit(solution)/shard_map/pallas_call | solution.py:338
  106.1 1.8 %collective-permute-start.7 = (bf16[64,1024]{1,0:T(8,128)(2,1)}, bf16[64,1024]{1,0:T(8,128)(2,1)S(1)}, u32[]{:S(2)}, u32[]{:S(2)}) collective-permute-start(bf16[64,1024]{1,0:T(8,128)(2,1)} %get-tuple-element.30), channel_id=1, source_target_pairs={{0,224},{32,0},{64,32},{96,64},{128,96},{160,128},{192,160},{224,1... | collective-permute-start | bytes 393224 | tf_op jit(solution)/shard_map/ppermute | solution.py:206
  107.9 3.1 %collective-permute-done.6.refs_0_ = bf16[64,1024]{1,0:T(8,128)(2,1)S(1)} collective-permute-done((bf16[64,1024]{1,0:T(8,128)(2,1)}, bf16[64,1024]{1,0:T(8,128)(2,1)S(1)}, u32[]{:S(2)}, u32[]{:S(2)}) %collective-permute-start.6) | collective-permute-done | bytes 131104 | tf_op jit(solution)/shard_map/ppermute | solution.py:206
  111.3 2.0 %ring_add.3 = (bf16[128,1024]{1,0:T(8,128)(2,1)}, bf16[128,1024]{1,0:T(8,128)(2,1)}) custom-call(bf16[64,1024]{1,0:T(8,128)(2,1)S(1)} %collective-permute-done.6.refs_0_, bf16[64,1024]{1,0:T(8,128)(2,1)S(1)} %collective-permute-done.7.refs_1_, f32[128,1024]{1,0:T(8,128)} %get-tuple-element.32.refs_2_, f32[128,1024]{1,0:T(8,128)} %get-tuple-element.33.refs_3_), custom_call_target="tpu_custom_call" | custom-call | tf_op jit(solution)/shard_map/ring_add/pallas_call | solution.py:240
  113.3 1.5 %collective-permute-start.8 = (bf16[128,1024]{1,0:T(8,128)(2,1)}, bf16[128,1024]{1,0:T(8,128)(2,1)S(1)}, u32[]{:S(2)}, u32[]{:S(2)}) collective-permute-start(bf16[128,1024]{1,0:T(8,128)(2,1)} %get-tuple-element.34), channel_id=1, source_target_pairs={{0,32},{32,64},{64,96},{96,128},{128,160},{160,192},{192,224},{224... | collective-permute-start | bytes 786440 | tf_op jit(solution)/shard_map/ppermute | solution.py:206
  114.8 1.8 %collective-permute-start.9 = (bf16[128,1024]{1,0:T(8,128)(2,1)}, bf16[128,1024]{1,0:T(8,128)(2,1)S(1)}, u32[]{:S(2)}, u32[]{:S(2)}) collective-permute-start(bf16[128,1024]{1,0:T(8,128)(2,1)} %get-tuple-element.35), channel_id=1, source_target_pairs={{0,224},{32,0},{64,32},{96,64},{128,96},{160,128},{192,160},{224,1... | collective-permute-start | bytes 786440 | tf_op jit(solution)/shard_map/ppermute | solution.py:206
  116.6 4.6 %collective-permute-done.8.refs_0_ = bf16[128,1024]{1,0:T(8,128)(2,1)S(1)} collective-permute-done((bf16[128,1024]{1,0:T(8,128)(2,1)}, bf16[128,1024]{1,0:T(8,128)(2,1)S(1)}, u32[]{:S(2)}, u32[]{:S(2)}) %collective-permute-start.8) | collective-permute-done | bytes 262176 | tf_op jit(solution)/shard_map/ppermute | solution.py:206
  121.5 2.0 %ring_add.4 = (bf16[128,1024]{1,0:T(8,128)(2,1)}, bf16[128,1024]{1,0:T(8,128)(2,1)}) custom-call(bf16[128,1024]{1,0:T(8,128)(2,1)S(1)} %collective-permute-done.8.refs_0_, bf16[128,1024]{1,0:T(8,128)(2,1)S(1)} %collective-permute-done.9.refs_1_, f32[128,1024]{1,0:T(8,128)} %get-tuple-element.36.refs_2_, f32[128,1024]{1,0:T(8,128)} %get-tuple-element.37.refs_3_), custom_call_target="tpu_custom_call" | custom-call | tf_op jit(solution)/shard_map/ring_add/pallas_call | solution.py:240
  123.5 3.3 %collective-permute-start.10 = (bf16[128,1024]{1,0:T(8,128)(2,1)}, bf16[128,1024]{1,0:T(8,128)(2,1)S(1)}, u32[]{:S(2)}, u32[]{:S(2)}) collective-permute-start(bf16[128,1024]{1,0:T(8,128)(2,1)} %get-tuple-element.38), channel_id=1, source_target_pairs={{0,32},{32,64},{64,96},{96,128},{128,160},{160,192},{192,224},{224... | collective-permute-start | bytes 786440 | tf_op jit(solution)/shard_map/ppermute | solution.py:206
  126.8 4.6 %collective-permute-done.10.refs_0_ = bf16[128,1024]{1,0:T(8,128)(2,1)S(1)} collective-permute-done((bf16[128,1024]{1,0:T(8,128)(2,1)}, bf16[128,1024]{1,0:T(8,128)(2,1)S(1)}, u32[]{:S(2)}, u32[]{:S(2)}) %collective-permute-start.10) | collective-permute-done | bytes 262176 | tf_op jit(solution)/shard_map/ppermute | solution.py:206
  131.4 2.0 %collective-permute-done.11.refs_1_ = bf16[128,1024]{1,0:T(8,128)(2,1)S(1)} collective-permute-done((bf16[128,1024]{1,0:T(8,128)(2,1)}, bf16[128,1024]{1,0:T(8,128)(2,1)S(1)}, u32[]{:S(2)}, u32[]{:S(2)}) %collective-permute-start.11) | collective-permute-done | bytes 262176 | tf_op jit(solution)/shard_map/ppermute | solution.py:206
  133.4 2.0 %ring_add.5 = (bf16[128,1024]{1,0:T(8,128)(2,1)}, bf16[128,1024]{1,0:T(8,128)(2,1)}) custom-call(bf16[128,1024]{1,0:T(8,128)(2,1)S(1)} %collective-permute-done.10.refs_0_, bf16[128,1024]{1,0:T(8,128)(2,1)S(1)} %collective-permute-done.11.refs_1_, f32[128,1024]{1,0:T(8,128)} %get-tuple-element.40.refs_2_, f32[128,1024]{1,0:T(8,128)} %get-tuple-element.41.refs_3_), custom_call_target="tpu_custom_call" | custom-call | tf_op jit(solution)/shard_map/ring_add/pallas_call | solution.py:240
  135.4 2.1 %collective-permute-start.12 = (bf16[128,1024]{1,0:T(8,128)(2,1)}, bf16[128,1024]{1,0:T(8,128)(2,1)S(1)}, u32[]{:S(2)}, u32[]{:S(2)}) collective-permute-start(bf16[128,1024]{1,0:T(8,128)(2,1)} %get-tuple-element.42), channel_id=1, source_target_pairs={{0,32},{32,64},{64,96},{96,128},{128,160},{160,192},{192,224},{224... | collective-permute-start | bytes 786440 | tf_op jit(solution)/shard_map/ppermute | solution.py:206
  139.4 5.4 %fields.1 = f32[2,2,1,8,8192]{4,3,2,1,0:T(8,128)} custom-call(f32[12,8,32]{2,1,0:T(8,128)} %bitcast.17, s32[1,32]{1,0:T(1,128)} %bitcast.21, f32[64,1024]{1,0:T(8,128)} %multiply_cosine_fusion.wave_ref), custom_call_target="tpu_custom_call" | custom-call | tf_op jit(solution)/shard_map/fields/pallas_call | solution.py:194
  144.8 1.9 %maps.1 = f32[2,1,8,8192]{3,2,1,0:T(8,128)} custom-call(f32[128,1024]{1,0:T(8,128)} %get-tuple-element.28.own, bf16[128,1024]{1,0:T(8,128)(2,1)S(1)} %collective-permute-done.12.up, bf16[128,1024]{1,0:T(8,128)(2,1)S(1)} %collective-permute-done.13.down), custom_call_target="tpu_custom_call" | custom-call | tf_op jit(solution)/shard_map/maps/pallas_call | solution.py:386
  (36 shorter events, 7.9 us)
Async XLA Ops:
  6.2 30.4 %collective-permute-start.2 = (bf16[528,1024]{1,0:T(8,128)(2,1)}, bf16[528,1024]{1,0:T(8,128)(2,1)S(1)}, u32[]{:S(2)}, u32[]{:S(2)}) collective-permute-start(bf16[528,1024]{1,0:T(8,128)(2,1)} %get-tuple-element.26.refs_1_.refs_3_), channel_id=1, source_target_pairs={{0,24},{8,0},{16,8},{24,16},{1,25},{9,1},{17,9},{25,17},{2,26},{10... | collective-permute-start | bytes 3244040 | tf_op jit(solution)/shard_map/ppermute | solution.py:206
  8.4 18.6 %copy-start.2 = (bf16[528,1024]{1,0:T(8,128)(2,1)S(1)}, bf16[528,1024]{1,0:T(8,128)(2,1)}, u32[]{:S(2)}) copy-start(bf16[528,1024]{1,0:T(8,128)(2,1)} %get-tuple-element.23.refs_0_.refs_2_) | copy-start | bytes 3244036
  8.4 30.9 %collective-permute-start = (bf16[528,1024]{1,0:T(8,128)(2,1)}, bf16[528,1024]{1,0:T(8,128)(2,1)S(1)}, u32[]{:S(2)}, u32[]{:S(2)}) collective-permute-start(bf16[528,1024]{1,0:T(8,128)(2,1)} %get-tuple-element.23.refs_0_.refs_2_), channel_id=1, source_target_pairs={{0,8},{8,16},{16,24},{24,0},{1,9},{9,17},{17,25},{25,1},{2,10},{10... | collective-permute-start | bytes 3244040 | tf_op jit(solution)/shard_map/ppermute | solution.py:206
  12.9 23.8 %all-to-all-start = ((f32[32,8,128]{2,1,0:T(8,128)}), f32[32,8,128]{2,1,0:T(8,128)S(1)}, u32[]{:S(2)}, u32[]{:S(2)}) async-start(f32[32,8,128]{2,1,0:T(8,128)} %modes.1), calls=%async_computation | async-start | bytes 262144 | tf_op jit(solution)/shard_map/all_to_all | solution.py:405
  25.4 65.4 %collective-permute-start.4 = (bf16[528,1024]{1,0:T(8,128)(2,1)}, bf16[528,1024]{1,0:T(8,128)(2,1)}, u32[]{:S(2)}, u32[]{:S(2)}) collective-permute-start(bf16[528,1024]{1,0:T(8,128)(2,1)} %get-tuple-element.26.refs_1_.refs_3_), channel_id=1, source_target_pairs={{0,8},{8,16},{16,24},{24,0},{1,9},{9,17},{17,25},{25,1},{2,10},{10... | collective-permute-start | bytes 3244040 | tf_op jit(solution)/shard_map/ppermute | solution.py:206
  27.0 63.8 %collective-permute-start.5 = (bf16[528,1024]{1,0:T(8,128)(2,1)S(1)}, bf16[528,1024]{1,0:T(8,128)(2,1)}, u32[]{:S(2)}, u32[]{:S(2)}) collective-permute-start(bf16[528,1024]{1,0:T(8,128)(2,1)S(1)} %copy-done.2), channel_id=1, source_target_pairs={{0,24},{8,0},{16,8},{24,16},{1,25},{9,1},{17,9},{25,17},{2,26},{10... | collective-permute-start | bytes 3244040 | tf_op jit(solution)/shard_map/ppermute | solution.py:206
  36.7 18.4 %copy-start = (bf16[528,1024]{1,0:T(8,128)(2,1)}, bf16[528,1024]{1,0:T(8,128)(2,1)S(1)}, u32[]{:S(2)}) copy-start(bf16[528,1024]{1,0:T(8,128)(2,1)S(1)} %collective-permute-done.2.refs_1_.refs_3_) | copy-start | bytes 3244036
  36.7 61.3 %collective-permute-start.3 = (bf16[528,1024]{1,0:T(8,128)(2,1)S(1)}, bf16[528,1024]{1,0:T(8,128)(2,1)}, u32[]{:S(2)}, u32[]{:S(2)}) collective-permute-start(bf16[528,1024]{1,0:T(8,128)(2,1)S(1)} %collective-permute-done.2.refs_1_.refs_3_), channel_id=1, source_target_pairs={{0,24},{8,0},{16,8},{24,16},{1,25},{9,1},{17,9},{25,17},{2,26},{10... | collective-permute-start | bytes 3244040 | tf_op jit(solution)/shard_map/ppermute | solution.py:206
  39.3 15.8 %copy-start.1 = (bf16[528,1024]{1,0:T(8,128)(2,1)}, bf16[528,1024]{1,0:T(8,128)(2,1)S(1)}, u32[]{:S(2)}) copy-start(bf16[528,1024]{1,0:T(8,128)(2,1)S(1)} %collective-permute-done.refs_0_.refs_2_) | copy-start | bytes 3244036
  39.3 58.6 %collective-permute-start.1 = (bf16[528,1024]{1,0:T(8,128)(2,1)S(1)}, bf16[528,1024]{1,0:T(8,128)(2,1)}, u32[]{:S(2)}, u32[]{:S(2)}) collective-permute-start(bf16[528,1024]{1,0:T(8,128)(2,1)S(1)} %collective-permute-done.refs_0_.refs_2_), channel_id=1, source_target_pairs={{0,8},{8,16},{16,24},{24,0},{1,9},{9,17},{17,25},{25,1},{2,10},{10... | collective-permute-start | bytes 3244040 | tf_op jit(solution)/shard_map/ppermute | solution.py:206
  40.0 9.7 %all-to-all-start.1 = ((bf16[8,8,128]{2,1,0:T(8,128)(2,1)}), bf16[8,8,128]{2,1,0:T(8,128)(2,1)S(1)}, u32[]{:S(2)}, u32[]{:S(2)}) async-start(bf16[8,8,128]{2,1,0:T(8,128)(2,1)} %harmonics.1), calls=%async_computation.1 | async-start | bytes 32768 | tf_op jit(solution)/shard_map/all_to_all | solution.py:408
  55.1 9.4 %all-to-all-start.2 = ((f32[8,12,256]{2,1,0:T(8,128)}), f32[8,12,256]{2,1,0:T(8,128)S(1)}, u32[]{:S(2)}, u32[]{:S(2)}) async-start(f32[8,12,256]{2,1,0:T(8,128)} %legendre.1), calls=%async_computation.2 | async-start | bytes 262144 | tf_op jit(solution)/shard_map/all_to_all | solution.py:411
  65.5 42.4 %all-to-all-start.3 = ((bf16[32,1,96]{2,1,0:T(2,128)(2,1)}), bf16[32,1,96]{2,1,0:T(2,128)(2,1)S(1)}, u32[]{:S(2)}, u32[]{:S(2)}) async-start(bf16[32,1,96]{2,1,0:T(2,128)(2,1)} %copy.14), calls=%async_computation.3 | async-start | bytes 32768 | tf_op jit(solution)/shard_map/all_to_all | solution.py:414
  104.6 6.5 %collective-permute-start.6 = (bf16[64,1024]{1,0:T(8,128)(2,1)}, bf16[64,1024]{1,0:T(8,128)(2,1)S(1)}, u32[]{:S(2)}, u32[]{:S(2)}) collective-permute-start(bf16[64,1024]{1,0:T(8,128)(2,1)} %get-tuple-element.29), channel_id=1, source_target_pairs={{0,32},{32,64},{64,96},{96,128},{128,160},{160,192},{192,224},{224... | collective-permute-start | bytes 393224 | tf_op jit(solution)/shard_map/ppermute | solution.py:206
  106.1 5.2 %collective-permute-start.7 = (bf16[64,1024]{1,0:T(8,128)(2,1)}, bf16[64,1024]{1,0:T(8,128)(2,1)S(1)}, u32[]{:S(2)}, u32[]{:S(2)}) collective-permute-start(bf16[64,1024]{1,0:T(8,128)(2,1)} %get-tuple-element.30), channel_id=1, source_target_pairs={{0,224},{32,0},{64,32},{96,64},{128,96},{160,128},{192,160},{224,1... | collective-permute-start | bytes 393224 | tf_op jit(solution)/shard_map/ppermute | solution.py:206
  113.3 7.9 %collective-permute-start.8 = (bf16[128,1024]{1,0:T(8,128)(2,1)}, bf16[128,1024]{1,0:T(8,128)(2,1)S(1)}, u32[]{:S(2)}, u32[]{:S(2)}) collective-permute-start(bf16[128,1024]{1,0:T(8,128)(2,1)} %get-tuple-element.34), channel_id=1, source_target_pairs={{0,32},{32,64},{64,96},{96,128},{128,160},{160,192},{192,224},{224... | collective-permute-start | bytes 786440 | tf_op jit(solution)/shard_map/ppermute | solution.py:206
  114.8 6.7 %collective-permute-start.9 = (bf16[128,1024]{1,0:T(8,128)(2,1)}, bf16[128,1024]{1,0:T(8,128)(2,1)S(1)}, u32[]{:S(2)}, u32[]{:S(2)}) collective-permute-start(bf16[128,1024]{1,0:T(8,128)(2,1)} %get-tuple-element.35), channel_id=1, source_target_pairs={{0,224},{32,0},{64,32},{96,64},{128,96},{160,128},{192,160},{224,1... | collective-permute-start | bytes 786440 | tf_op jit(solution)/shard_map/ppermute | solution.py:206
  123.5 7.9 %collective-permute-start.10 = (bf16[128,1024]{1,0:T(8,128)(2,1)}, bf16[128,1024]{1,0:T(8,128)(2,1)S(1)}, u32[]{:S(2)}, u32[]{:S(2)}) collective-permute-start(bf16[128,1024]{1,0:T(8,128)(2,1)} %get-tuple-element.38), channel_id=1, source_target_pairs={{0,32},{32,64},{64,96},{96,128},{128,160},{160,192},{192,224},{224... | collective-permute-start | bytes 786440 | tf_op jit(solution)/shard_map/ppermute | solution.py:206
  126.8 6.6 %collective-permute-start.11 = (bf16[128,1024]{1,0:T(8,128)(2,1)}, bf16[128,1024]{1,0:T(8,128)(2,1)S(1)}, u32[]{:S(2)}, u32[]{:S(2)}) collective-permute-start(bf16[128,1024]{1,0:T(8,128)(2,1)} %get-tuple-element.39), channel_id=1, source_target_pairs={{0,224},{32,0},{64,32},{96,64},{128,96},{160,128},{192,160},{224,1... | collective-permute-start | bytes 786440 | tf_op jit(solution)/shard_map/ppermute | solution.py:206
  135.4 9.4 %collective-permute-start.12 = (bf16[128,1024]{1,0:T(8,128)(2,1)}, bf16[128,1024]{1,0:T(8,128)(2,1)S(1)}, u32[]{:S(2)}, u32[]{:S(2)}) collective-permute-start(bf16[128,1024]{1,0:T(8,128)(2,1)} %get-tuple-element.42), channel_id=1, source_target_pairs={{0,32},{32,64},{64,96},{96,128},{128,160},{160,192},{192,224},{224... | collective-permute-start | bytes 786440 | tf_op jit(solution)/shard_map/ppermute | solution.py:206
  137.5 7.3 %collective-permute-start.13 = (bf16[128,1024]{1,0:T(8,128)(2,1)}, bf16[128,1024]{1,0:T(8,128)(2,1)S(1)}, u32[]{:S(2)}, u32[]{:S(2)}) collective-permute-start(bf16[128,1024]{1,0:T(8,128)(2,1)} %get-tuple-element.43), channel_id=1, source_target_pairs={{0,224},{32,0},{64,32},{96,64},{128,96},{160,128},{192,160},{224,1... | collective-permute-start | bytes 786440 | tf_op jit(solution)/shard_map/ppermute | solution.py:206
where the time goes:
time: 148 us; the launch traced here: 147 us
  Pallas kernels  54 us (36%)
  starting transfers between devices  51.6 us (35%)
  waiting for transfers between devices  35.4 us (24%)
  local copies, waits for them, and re-layouts  2.57 us (2%)
  other arithmetic  2.31 us (2%)
    pallas_call x4, Pallas kernels, sum_pieces(): pl.pallas_call(functools.partial(sums_kernel, len(pieces), int(base is no...  27.1 us
    ppermute x14, starting transfers between devices, shifted(): return lax.ppermute(x, axis, [(i, (i + by) % size) for i in range(size)])  20.1 us
    ppermute x14, waiting for transfers between devices, shifted(): return lax.ppermute(x, axis, [(i, (i + by) % size) for i in range(size)])  14.9 us
    all_to_all x1, starting transfers between devices, body(): arrived = lax.all_to_all(sums, BLK, split_axis=0, concat_axis=0, tiled=True)  12.5 us
    all_to_all x1, starting transfers between devices, body(): lax.all_to_all(summed, BLK, split_axis=0, concat_axis=0, tiled=True)  11.3 us
    all_to_all x1, waiting for transfers between devices, body(): arrived = lax.all_to_all(sums, BLK, split_axis=0, concat_axis=0, tiled=True)  9.13 us
    all_to_all x1, waiting for transfers between devices, body(): lax.all_to_all(pieces, 'lblk', split_axis=0, concat_axis=0, tiled=True)  6.02 us
    pallas_call x3, Pallas kernels, ring_add(): pl.pallas_call(add_kernel, out_shape=(result, result), in_specs=[vmem, vm...  5.93 us
  transfers between devices with their start and end apart: 18, of which 9 were waited for; matrix products, arithmetic and copies ran while one was open for 2% of the time, Pallas kernels for 29%

commit v1 on v0

--- a/solution.py
+++ b/solution.py
@@ -21,6 +21,10 @@
 
 NT = (((1,), (1,)), ((), ()))
 NN = (((1,), (0,)), ((), ()))
+
+
+def room(mebibytes):
+    return pltpu.CompilerParams(vmem_limit_bytes=mebibytes << 20)
 
 
 def halves(x):
@@ -198,6 +202,7 @@
         in_specs=[whole(12, R_DEV, orders), whole(1, orders), whole(2 * orders, SEG)],
         out_specs=pl.BlockSpec((2, 2, 1, R_DEV, SEG), lambda p: (0, 0, 0, 0, p)),
         name="fields",
+        compiler_params=room(16),
     )(terms, azimuth_orders[None], waves)
 
 
@@ -206,47 +211,34 @@
     return lax.ppermute(x, axis, [(i, (i + by) % size) for i in range(size)])
 
 
-def add_kernel(*refs):
-    moving, own_hbm, out_hbm = refs[:2], refs[2:4], refs[4:6]
-    own, result, sems = refs[6:8], refs[8:10], refs[10]
-    size, whole = moving[0].shape[0], own[0].shape[0]
-    copies = []
-    for side in range(2):
-        copies.append(pltpu.make_async_copy(own_hbm[side], own[side], sems.at[side]))
-        copies[-1].start()
-    sent = []
-    for side, lead in ((0, 0), (1, whole - size)):
-        copies[side].wait()
+def add_kernel(up_ref, down_ref, up_own_ref, down_own_ref, up_out, down_out):
+    size, whole = up_ref.shape[0], up_own_ref.shape[0]
+    for lead, moving_ref, own_ref, out in (
+        (0, up_ref, up_own_ref, up_out),
+        (whole - size, down_ref, down_own_ref, down_out),
+    ):
         if size < whole:
             other = size - lead
-            kept = own[side][other : other + size]
-            result[side][other : other + size] = kept.astype(result[side].dtype)
-        added = own[side][lead : lead + size] + moving[side][...].astype(jnp.float32)
-        result[side][lead : lead + size] = added.astype(result[side].dtype)
-        sent.append(pltpu.make_async_copy(result[side], out_hbm[side], sems.at[2 + side]))
-        sent[-1].start()
-    for copy in sent:
-        copy.wait()
+            out[other : other + size] = own_ref[other : other + size].astype(out.dtype)
+        added = own_ref[lead : lead + size] + moving_ref[...].astype(jnp.float32)
+        out[lead : lead + size] = added.astype(out.dtype)
 
 
 def in_vmem(x):
     return pltpu.with_memory_space_constraint(x, pltpu.VMEM)
 
 
-def ring_add(up, down, up_own, down_own):
+def ring_add(*operands):
     vmem = pl.BlockSpec(memory_space=pltpu.VMEM)
-    hbm = pl.BlockSpec(memory_space=pltpu.HBM)
-    result = jax.ShapeDtypeStruct(up_own.shape, up.dtype)
+    result = pltpu.VMEM(operands[2].shape, operands[0].dtype)
     return pl.pallas_call(
         add_kernel,
         out_shape=(result, result),
-        in_specs=[vmem, vmem, hbm, hbm],
-        out_specs=(hbm, hbm),
-        scratch_shapes=[pltpu.VMEM(up_own.shape, up_own.dtype)] * 2
-        + [pltpu.VMEM(up_own.shape, up.dtype)] * 2
-        + [pltpu.SemaphoreType.DMA((4,))],
+        in_specs=[vmem] * 4,
+        out_specs=(vmem, vmem),
         name="ring_add",
-    )(in_vmem(up), in_vmem(down), up_own, down_own)
+        compiler_params=room(8),
+    )(*[in_vmem(x) if x.shape == operands[0].shape else x for x in operands])
 
 
 def ring_sums(chunks, far, axis, token):
@@ -388,7 +380,8 @@
         out_shape=jax.ShapeDtypeStruct((2, 1, R_DEV, NPHI), jnp.float32),
         in_specs=[vmem] * 3,
         name="maps",
-    )(own, in_vmem(up), in_vmem(down))
+        compiler_params=room(8),
+    )(in_vmem(own), in_vmem(up), in_vmem(down))
 
 
 def body(partial_rows, row_owner, row_key, azimuth_orders, legendre_table, spin_even, spin_odd):

time: 148 us -> 143 us (0.966)
  Pallas kernels: 54 us -> 46.3 us
  local copies, waits for them, and re-layouts: 2.57 us -> 4.06 us
    pallas_call x3, Pallas kernels: 5.93 us -> 0.27 us  [ring_add(): pl.pallas_call(add_kernel, out_shape=(result, result), in_specs=[vmem] *...]
    unnamed x6 -> x24, local copies, waits for them, and re-layouts: 0.01 us -> 2.13 us
  transfers between devices with their start and end apart: 18 -> 18, of which waited for: 9 -> 10; matrix products, arithmetic and copies ran while one was open for 2% -> 1% of each run, Pallas kernels for 29% -> 30%
where the time goes in v1:
time: 143 us; the launch traced here: 142 us
  starting transfers between devices  51.6 us (36%)
  Pallas kernels  46.3 us (32%)
  waiting for transfers between devices  36.7 us (26%)
  local copies, waits for them, and re-layouts  4.06 us (3%)
  other arithmetic  2.31 us (2%)
    pallas_call x4, Pallas kernels, sum_pieces(): pl.pallas_call(functools.partial(sums_kernel, len(pieces), int(base is no...  27.1 us
    ppermute x14, starting transfers between devices, shifted(): return lax.ppermute(x, axis, [(i, (i + by) % size) for i in range(size)])  20.1 us
    ppermute x14, waiting for transfers between devices, shifted(): return lax.ppermute(x, axis, [(i, (i + by) % size) for i in range(size)])  16.2 us
    all_to_all x1, starting transfers between devices, body(): arrived = lax.all_to_all(sums, BLK, split_axis=0, concat_axis=0, tiled=True)  12.5 us
    all_to_all x1, starting transfers between devices, body(): lax.all_to_all(summed, BLK, split_axis=0, concat_axis=0, tiled=True)  11.3 us
    all_to_all x1, waiting for transfers between devices, body(): arrived = lax.all_to_all(sums, BLK, split_axis=0, concat_axis=0, tiled=True)  9.13 us
    all_to_all x1, waiting for transfers between devices, body(): lax.all_to_all(pieces, 'lblk', split_axis=0, concat_axis=0, tiled=True)  6.02 us
    pallas_call x1, Pallas kernels, legendre_pair(): pl.pallas_call(legendre_kernel, out_shape=jax.ShapeDtypeStruct((blocks, 1...  5.41 us
  transfers between devices with their start and end apart: 18, of which 10 were waited for; matrix products, arithmetic and copies ran while one was open for 1% of the time, Pallas kernels for 30%

profile of v1, /device:TPU:8, one launch (start us, length us, event | category | flops | bytes accessed | tf_op | source)
XLA Modules:
  0.0 141.9 jit_solution(8163613058900214463)
XLA Ops:
  1.5 1.7 %multiply_cosine_fusion.wave_ref = f32[64,1024]{1,0:T(8,128)} fusion(s32[64]{0:T(128)S(1)} %iota.19, s32[64]{0:T(128)S(1)} %mul.32), kind=kLoop, calls=%fused_computation | loop fusion | flops 327680 | bytes 262656 | tf_op jit(solution)/shard_map/cos | solution.py:46
  3.2 3.0 %pack.1 = (bf16[528,1024]{1,0:T(8,128)(2,1)}, bf16[528,1024]{1,0:T(8,128)(2,1)}) custom-call(bf16[1024,1024]{1,0:T(8,128)(2,1)} %bitcast.16, s32[1,1024]{1,0:T(1,128)} %bitcast.20, s32[1,1024]{1,0:T(1,128)} %key_ref.3), custom_call_target="tpu_custom_call" | custom-call | tf_op jit(solution)/shard_map/pack/pallas_call | solution.py:284
  6.3 2.2 %collective-permute-start.2 = (bf16[528,1024]{1,0:T(8,128)(2,1)}, bf16[528,1024]{1,0:T(8,128)(2,1)S(1)}, u32[]{:S(2)}, u32[]{:S(2)}) collective-permute-start(bf16[528,1024]{1,0:T(8,128)(2,1)} %get-tuple-element.26.refs_1_.refs_3_), channel_id=1, source_target_pairs={{0,24},{8,0},{16,8},{24,16},{1,25},{9,1},{17,9},{25,17},{2,26},{10... | collective-permute-start | bytes 3244040 | tf_op jit(solution)/shard_map/ppermute | solution.py:211
  8.4 4.5 %modes.1 = f32[32,8,128]{2,1,0:T(8,128)} custom-call(bf16[1024,1024]{1,0:T(8,128)(2,1)} %bitcast.17, s32[1,1024]{1,0:T(1,128)} %bitcast.21, s32[1,1024]{1,0:T(1,128)} %key_ref.3, f32[64,1024]{1,0:T(8,128)} %multiply_cosine_fusion.wave_ref), custom_call_target="tpu_custom_call" | custom-call | tf_op jit(solution)/shard_map/modes/pallas_call | solution.py:91
  12.9 12.5 %all-to-all-start = ((f32[32,8,128]{2,1,0:T(8,128)}), f32[32,8,128]{2,1,0:T(8,128)S(1)}, u32[]{:S(2)}, u32[]{:S(2)}) async-start(f32[32,8,128]{2,1,0:T(8,128)} %modes.1), calls=%async_computation | async-start | bytes 262144 | tf_op jit(solution)/shard_map/all_to_all | solution.py:398
  25.4 1.5 %collective-permute-start.4 = (bf16[528,1024]{1,0:T(8,128)(2,1)}, bf16[528,1024]{1,0:T(8,128)(2,1)}, u32[]{:S(2)}, u32[]{:S(2)}) collective-permute-start(bf16[528,1024]{1,0:T(8,128)(2,1)} %get-tuple-element.26.refs_1_.refs_3_), channel_id=1, source_target_pairs={{0,8},{8,16},{16,24},{24,0},{1,9},{9,17},{17,25},{25,1},{2,10},{10... | collective-permute-start | bytes 3244040 | tf_op jit(solution)/shard_map/ppermute | solution.py:211
  27.6 9.1 %all-to-all-done.in_ref = f32[32,8,128]{2,1,0:T(8,128)S(1)} async-done(((f32[32,8,128]{2,1,0:T(8,128)}), f32[32,8,128]{2,1,0:T(8,128)S(1)}, u32[]{:S(2)}, u32[]{:S(2)}) %all-to-all-start) | async-done | bytes 131104 | tf_op jit(solution)/shard_map/all_to_all | solution.py:398
  36.7 2.6 %collective-permute-start.3 = (bf16[528,1024]{1,0:T(8,128)(2,1)S(1)}, bf16[528,1024]{1,0:T(8,128)(2,1)}, u32[]{:S(2)}, u32[]{:S(2)}) collective-permute-start(bf16[528,1024]{1,0:T(8,128)(2,1)S(1)} %collective-permute-done.2.refs_1_.refs_3_), channel_id=1, source_target_pairs={{0,24},{8,0},{16,8},{24,16},{1,25},{9,1},{17,9},{25,17},{2,26},{10... | collective-permute-start | bytes 3244040 | tf_op jit(solution)/shard_map/ppermute | solution.py:211
  40.0 4.3 %all-to-all-start.1 = ((bf16[8,8,128]{2,1,0:T(8,128)(2,1)}), bf16[8,8,128]{2,1,0:T(8,128)(2,1)S(1)}, u32[]{:S(2)}, u32[]{:S(2)}) async-start(bf16[8,8,128]{2,1,0:T(8,128)(2,1)} %harmonics.1), calls=%async_computation.1 | async-start | bytes 32768 | tf_op jit(solution)/shard_map/all_to_all | solution.py:401
  44.3 5.4 %all-to-all-done.1.modes_ref = bf16[8,8,128]{2,1,0:T(8,128)(2,1)S(1)} async-done(((bf16[8,8,128]{2,1,0:T(8,128)(2,1)}), bf16[8,8,128]{2,1,0:T(8,128)(2,1)S(1)}, u32[]{:S(2)}, u32[]{:S(2)}) %all-to-all-start.1) | async-done | bytes 16416 | tf_op jit(solution)/shard_map/all_to_all | solution.py:401
  49.7 5.4 %legendre.1 = f32[8,12,256]{2,1,0:T(8,128)} custom-call(s32[1]{0:T(128)} %bitcast.first_ref, bf16[8,8,128]{2,1,0:T(8,128)(2,1)S(1)} %all-to-all-done.1.modes_ref, bf16[1,512,2048]{2,1,0:T(8,128)(2,1)} %leg_ref.1, bf16[1,512,2048]{2,1,0:T(8,128)(2,1)} %even_hbm.1, bf16[1,512,2048]{2,1,0:T(8,128)(2,1)} %odd_hbm.1), custom_call_target="tpu_custom_call" | custom-call | tf_op jit(solution)/shard_map/legendre/pallas_call | solution.py:155
  55.1 3.4 %all-to-all-start.2 = ((f32[8,12,256]{2,1,0:T(8,128)}), f32[8,12,256]{2,1,0:T(8,128)S(1)}, u32[]{:S(2)}, u32[]{:S(2)}) async-start(f32[8,12,256]{2,1,0:T(8,128)} %legendre.1), calls=%async_computation.2 | async-start | bytes 262144 | tf_op jit(solution)/shard_map/all_to_all | solution.py:404
  58.5 6.0 %all-to-all-done.2 = f32[8,12,256]{2,1,0:T(8,128)S(1)} async-done(((f32[8,12,256]{2,1,0:T(8,128)}), f32[8,12,256]{2,1,0:T(8,128)S(1)}, u32[]{:S(2)}, u32[]{:S(2)}) %all-to-all-start.2) | async-done | bytes 98336 | tf_op jit(solution)/shard_map/all_to_all | solution.py:404
  65.5 11.3 %all-to-all-start.3 = ((bf16[32,1,96]{2,1,0:T(2,128)(2,1)}), bf16[32,1,96]{2,1,0:T(2,128)(2,1)S(1)}, u32[]{:S(2)}, u32[]{:S(2)}) async-start(bf16[32,1,96]{2,1,0:T(2,128)(2,1)} %copy.14), calls=%async_computation.3 | async-start | bytes 32768 | tf_op jit(solution)/shard_map/all_to_all | solution.py:407
  77.4 6.2 %shard_map.86.refs_4_ = f32[1024,1024]{1,0:T(8,128)} custom-call(s32[2]{0:T(128)} %pad_add_fusion.place_ref, bf16[528,1024]{1,0:T(8,128)(2,1)} %get-tuple-element.23.refs_0_.refs_2_, bf16[528,1024]{1,0:T(8,128)(2,1)} %get-tuple-element.26.refs_1_.refs_3_, bf16[528,1024]{1,0:T(8,128)(2,1)} %get-tuple-element.23.refs_0_.refs_2_, ...), custom_call_target="tpu_custom_call" | custom-call | tf_op jit(solution)/shard_map/pallas_call | solution.py:330
  83.6 7.2 %shard_map.87.refs_4_ = f32[1024,1024]{1,0:T(8,128)} custom-call(s32[2]{0:T(128)} %pad_add_fusion.place_ref, bf16[528,1024]{1,0:T(8,128)(2,1)} %copy-done.10, bf16[528,1024]{1,0:T(8,128)(2,1)} %copy-done.9, bf16[528,1024]{1,0:T(8,128)(2,1)} %copy-done.10, bf16[528,1024]{1,0:T(8,128)(2,1)} %copy-done.9, f32[1024,1024]{1,0:T(8,128)} %shard_map.86.refs_4_), custom_call_target="tpu_custom_call" | custom-call | tf_op jit(solution)/shard_map/pallas_call | solution.py:330
  90.8 7.1 %shard_map.88.refs_4_ = f32[1024,1024]{1,0:T(8,128)} custom-call(s32[2]{0:T(128)} %pad_add_fusion.place_ref, bf16[528,1024]{1,0:T(8,128)(2,1)} %collective-permute-done.4.refs_0_.refs_2_, bf16[528,1024]{1,0:T(8,128)(2,1)} %collective-permute-done.5.refs_1_.refs_3_, bf16[528,1024]{1,0:T(8,128)(2,1)} %collective-permute-done.4.refs_0_.refs_2_, ...), custom_call_target="tpu_custom_call" | custom-call | tf_op jit(solution)/shard_map/pallas_call | solution.py:330
  97.9 6.6 %shard_map.89 = (f32[128,1024]{1,0:T(8,128)}, f32[128,1024]{1,0:T(8,128)}, f32[128,1024]{1,0:T(8,128)}, f32[128,1024]{1,0:T(8,128)}, bf16[64,1024]{1,0:T(8,128)(...) custom-call(s32[2]{0:T(128)} %pad_add_fusion.place_ref, ...), custom_call_target="tpu_custom_call" | custom-call | tf_op jit(solution)/shard_map/pallas_call | solution.py:330
  104.6 1.5 %collective-permute-start.6 = (bf16[64,1024]{1,0:T(8,128)(2,1)}, bf16[64,1024]{1,0:T(8,128)(2,1)S(1)}, u32[]{:S(2)}, u32[]{:S(2)}) collective-permute-start(bf16[64,1024]{1,0:T(8,128)(2,1)} %get-tuple-element.29), channel_id=1, source_target_pairs={{0,32},{32,64},{64,96},{96,128},{128,160},{160,192},{192,224},{224... | collective-permute-start | bytes 393224 | tf_op jit(solution)/shard_map/ppermute | solution.py:211
  106.1 1.8 %collective-permute-start.7 = (bf16[64,1024]{1,0:T(8,128)(2,1)}, bf16[64,1024]{1,0:T(8,128)(2,1)S(1)}, u32[]{:S(2)}, u32[]{:S(2)}) collective-permute-start(bf16[64,1024]{1,0:T(8,128)(2,1)} %get-tuple-element.30), channel_id=1, source_target_pairs={{0,224},{32,0},{64,32},{96,64},{128,96},{160,128},{192,160},{224,1... | collective-permute-start | bytes 393224 | tf_op jit(solution)/shard_map/ppermute | solution.py:211
  107.9 3.1 %collective-permute-done.6.up_ref = bf16[64,1024]{1,0:T(8,128)(2,1)S(1)} collective-permute-done((bf16[64,1024]{1,0:T(8,128)(2,1)}, bf16[64,1024]{1,0:T(8,128)(2,1)S(1)}, u32[]{:S(2)}, u32[]{:S(2)}) %collective-permute-start.6) | collective-permute-done | bytes 131104 | tf_op jit(solution)/shard_map/ppermute | solution.py:211
  111.3 1.0 copy-done.6
  112.4 1.0 copy-done.7
  113.5 1.5 %collective-permute-start.8 = (bf16[128,1024]{1,0:T(8,128)(2,1)S(1)}, bf16[128,1024]{1,0:T(8,128)(2,1)S(1)}, u32[]{:S(2)}, u32[]{:S(2)}) collective-permute-start(bf16[128,1024]{1,0:T(8,128)(2,1)S(1)} %get-tuple-element.34), channel_id=1, source_target_pairs={{0,32},{32,64},{64,96},{96,128},{128,160},{160,192},{192,224},{224... | collective-permute-start | bytes 786440 | tf_op jit(solution)/shard_map/ppermute | solution.py:211
  115.0 1.8 %collective-permute-start.9 = (bf16[128,1024]{1,0:T(8,128)(2,1)S(1)}, bf16[128,1024]{1,0:T(8,128)(2,1)S(1)}, u32[]{:S(2)}, u32[]{:S(2)}) collective-permute-start(bf16[128,1024]{1,0:T(8,128)(2,1)S(1)} %get-tuple-element.35), channel_id=1, source_target_pairs={{0,224},{32,0},{64,32},{96,64},{128,96},{160,128},{192,160},{224,1... | collective-permute-start | bytes 786440 | tf_op jit(solution)/shard_map/ppermute | solution.py:211
  116.8 4.3 %collective-permute-done.8.up_ref = bf16[128,1024]{1,0:T(8,128)(2,1)S(1)} collective-permute-done((bf16[128,1024]{1,0:T(8,128)(2,1)S(1)}, bf16[128,1024]{1,0:T(8,128)(2,1)S(1)}, u32[]{:S(2)}, u32[]{:S(2)}) %collective-permute-start.8) | collective-permute-done | bytes 262176 | tf_op jit(solution)/shard_map/ppermute | solution.py:211
  121.6 3.3 %collective-permute-start.10 = (bf16[128,1024]{1,0:T(8,128)(2,1)S(1)}, bf16[128,1024]{1,0:T(8,128)(2,1)S(1)}, u32[]{:S(2)}, u32[]{:S(2)}) collective-permute-start(bf16[128,1024]{1,0:T(8,128)(2,1)S(1)} %get-tuple-element.38), channel_id=1, source_target_pairs={{0,32},{32,64},{64,96},{96,128},{128,160},{160,192},{192,224},{224... | collective-permute-start | bytes 786440 | tf_op jit(solution)/shard_map/ppermute | solution.py:211
  124.9 4.3 %collective-permute-done.10.up_ref = bf16[128,1024]{1,0:T(8,128)(2,1)S(1)} collective-permute-done((bf16[128,1024]{1,0:T(8,128)(2,1)S(1)}, bf16[128,1024]{1,0:T(8,128)(2,1)S(1)}, u32[]{:S(2)}, u32[]{:S(2)}) %collective-permute-start.10) | collective-permute-done | bytes 262176 | tf_op jit(solution)/shard_map/ppermute | solution.py:211
  129.3 2.1 %collective-permute-done.11.down_ref = bf16[128,1024]{1,0:T(8,128)(2,1)S(1)} collective-permute-done((bf16[128,1024]{1,0:T(8,128)(2,1)S(1)}, bf16[128,1024]{1,0:T(8,128)(2,1)S(1)}, u32[]{:S(2)}, u32[]{:S(2)}) %collective-permute-start.11) | collective-permute-done | bytes 262176 | tf_op jit(solution)/shard_map/ppermute | solution.py:211
  131.5 3.1 %collective-permute-start.12 = (bf16[128,1024]{1,0:T(8,128)(2,1)S(1)}, bf16[128,1024]{1,0:T(8,128)(2,1)S(1)}, u32[]{:S(2)}, u32[]{:S(2)}) collective-permute-start(bf16[128,1024]{1,0:T(8,128)(2,1)S(1)} %get-tuple-element.42), channel_id=1, source_target_pairs={{0,32},{32,64},{64,96},{96,128},{128,160},{160,192},{192,224},{224... | collective-permute-start | bytes 786440 | tf_op jit(solution)/shard_map/ppermute | solution.py:211
  134.9 4.4 %fields.1 = f32[2,2,1,8,8192]{4,3,2,1,0:T(8,128)} custom-call(f32[12,8,32]{2,1,0:T(8,128)S(1)} %bitcast.14, s32[1,32]{1,0:T(1,128)S(1)} %bitcast.15, f32[64,1024]{1,0:T(8,128)S(1)} %copy-done), custom_call_target="tpu_custom_call" | custom-call | tf_op jit(solution)/shard_map/fields/pallas_call | solution.py:198
  139.3 1.7 %collective-permute-done.13.down = bf16[128,1024]{1,0:T(8,128)(2,1)S(1)} collective-permute-done((bf16[128,1024]{1,0:T(8,128)(2,1)S(1)}, bf16[128,1024]{1,0:T(8,128)(2,1)S(1)}, u32[]{:S(2)}, u32[]{:S(2)}) %collective-permute-start.13) | collective-permute-done | bytes 262176 | tf_op jit(solution)/shard_map/ppermute | solution.py:211
  (54 shorter events, 5.8 us)
Async XLA Ops:
  6.3 30.4 %collective-permute-start.2 = (bf16[528,1024]{1,0:T(8,128)(2,1)}, bf16[528,1024]{1,0:T(8,128)(2,1)S(1)}, u32[]{:S(2)}, u32[]{:S(2)}) collective-permute-start(bf16[528,1024]{1,0:T(8,128)(2,1)} %get-tuple-element.26.refs_1_.refs_3_), channel_id=1, source_target_pairs={{0,24},{8,0},{16,8},{24,16},{1,25},{9,1},{17,9},{25,17},{2,26},{10... | collective-permute-start | bytes 3244040 | tf_op jit(solution)/shard_map/ppermute | solution.py:211
  8.4 18.6 %copy-start.11 = (bf16[528,1024]{1,0:T(8,128)(2,1)S(1)}, bf16[528,1024]{1,0:T(8,128)(2,1)}, u32[]{:S(2)}) copy-start(bf16[528,1024]{1,0:T(8,128)(2,1)} %get-tuple-element.23.refs_0_.refs_2_) | copy-start | bytes 3244036
  8.4 30.9 %collective-permute-start = (bf16[528,1024]{1,0:T(8,128)(2,1)}, bf16[528,1024]{1,0:T(8,128)(2,1)S(1)}, u32[]{:S(2)}, u32[]{:S(2)}) collective-permute-start(bf16[528,1024]{1,0:T(8,128)(2,1)} %get-tuple-element.23.refs_0_.refs_2_), channel_id=1, source_target_pairs={{0,8},{8,16},{16,24},{24,0},{1,9},{9,17},{17,25},{25,1},{2,10},{10... | collective-permute-start | bytes 3244040 | tf_op jit(solution)/shard_map/ppermute | solution.py:211
  12.9 23.8 %all-to-all-start = ((f32[32,8,128]{2,1,0:T(8,128)}), f32[32,8,128]{2,1,0:T(8,128)S(1)}, u32[]{:S(2)}, u32[]{:S(2)}) async-start(f32[32,8,128]{2,1,0:T(8,128)} %modes.1), calls=%async_computation | async-start | bytes 262144 | tf_op jit(solution)/shard_map/all_to_all | solution.py:398
  25.4 65.3 %collective-permute-start.4 = (bf16[528,1024]{1,0:T(8,128)(2,1)}, bf16[528,1024]{1,0:T(8,128)(2,1)}, u32[]{:S(2)}, u32[]{:S(2)}) collective-permute-start(bf16[528,1024]{1,0:T(8,128)(2,1)} %get-tuple-element.26.refs_1_.refs_3_), channel_id=1, source_target_pairs={{0,8},{8,16},{16,24},{24,0},{1,9},{9,17},{17,25},{25,1},{2,10},{10... | collective-permute-start | bytes 3244040 | tf_op jit(solution)/shard_map/ppermute | solution.py:211
  27.0 63.8 %collective-permute-start.5 = (bf16[528,1024]{1,0:T(8,128)(2,1)S(1)}, bf16[528,1024]{1,0:T(8,128)(2,1)}, u32[]{:S(2)}, u32[]{:S(2)}) collective-permute-start(bf16[528,1024]{1,0:T(8,128)(2,1)S(1)} %copy-done.11), channel_id=1, source_target_pairs={{0,24},{8,0},{16,8},{24,16},{1,25},{9,1},{17,9},{25,17},{2,26},{10... | collective-permute-start | bytes 3244040 | tf_op jit(solution)/shard_map/ppermute | solution.py:211
  36.7 18.4 %copy-start.9 = (bf16[528,1024]{1,0:T(8,128)(2,1)}, bf16[528,1024]{1,0:T(8,128)(2,1)S(1)}, u32[]{:S(2)}) copy-start(bf16[528,1024]{1,0:T(8,128)(2,1)S(1)} %collective-permute-done.2.refs_1_.refs_3_) | copy-start | bytes 3244036
  36.7 61.2 %collective-permute-start.3 = (bf16[528,1024]{1,0:T(8,128)(2,1)S(1)}, bf16[528,1024]{1,0:T(8,128)(2,1)}, u32[]{:S(2)}, u32[]{:S(2)}) collective-permute-start(bf16[528,1024]{1,0:T(8,128)(2,1)S(1)} %collective-permute-done.2.refs_1_.refs_3_), channel_id=1, source_target_pairs={{0,24},{8,0},{16,8},{24,16},{1,25},{9,1},{17,9},{25,17},{2,26},{10... | collective-permute-start | bytes 3244040 | tf_op jit(solution)/shard_map/ppermute | solution.py:211
  39.3 15.8 %copy-start.10 = (bf16[528,1024]{1,0:T(8,128)(2,1)}, bf16[528,1024]{1,0:T(8,128)(2,1)S(1)}, u32[]{:S(2)}) copy-start(bf16[528,1024]{1,0:T(8,128)(2,1)S(1)} %collective-permute-done.refs_0_.refs_2_) | copy-start | bytes 3244036
  39.3 58.6 %collective-permute-start.1 = (bf16[528,1024]{1,0:T(8,128)(2,1)S(1)}, bf16[528,1024]{1,0:T(8,128)(2,1)}, u32[]{:S(2)}, u32[]{:S(2)}) collective-permute-start(bf16[528,1024]{1,0:T(8,128)(2,1)S(1)} %collective-permute-done.refs_0_.refs_2_), channel_id=1, source_target_pairs={{0,8},{8,16},{16,24},{24,0},{1,9},{9,17},{17,25},{25,1},{2,10},{10... | collective-permute-start | bytes 3244040 | tf_op jit(solution)/shard_map/ppermute | solution.py:211
  40.0 9.7 %all-to-all-start.1 = ((bf16[8,8,128]{2,1,0:T(8,128)(2,1)}), bf16[8,8,128]{2,1,0:T(8,128)(2,1)S(1)}, u32[]{:S(2)}, u32[]{:S(2)}) async-start(bf16[8,8,128]{2,1,0:T(8,128)(2,1)} %harmonics.1), calls=%async_computation.1 | async-start | bytes 32768 | tf_op jit(solution)/shard_map/all_to_all | solution.py:401
  55.1 9.4 %all-to-all-start.2 = ((f32[8,12,256]{2,1,0:T(8,128)}), f32[8,12,256]{2,1,0:T(8,128)S(1)}, u32[]{:S(2)}, u32[]{:S(2)}) async-start(f32[8,12,256]{2,1,0:T(8,128)} %legendre.1), calls=%async_computation.2 | async-start | bytes 262144 | tf_op jit(solution)/shard_map/all_to_all | solution.py:404
  65.5 42.4 %all-to-all-start.3 = ((bf16[32,1,96]{2,1,0:T(2,128)(2,1)}), bf16[32,1,96]{2,1,0:T(2,128)(2,1)S(1)}, u32[]{:S(2)}, u32[]{:S(2)}) async-start(bf16[32,1,96]{2,1,0:T(2,128)(2,1)} %copy.14), calls=%async_computation.3 | async-start | bytes 32768 | tf_op jit(solution)/shard_map/all_to_all | solution.py:407
  104.6 16.9 %copy-start.4 = (f32[128,1024]{1,0:T(8,128)S(1)}, f32[128,1024]{1,0:T(8,128)}, u32[]{:S(2)}) copy-start(f32[128,1024]{1,0:T(8,128)} %get-tuple-element.36.up_own_ref) | copy-start | bytes 1572868
  104.6 16.9 %copy-start.5 = (f32[128,1024]{1,0:T(8,128)S(1)}, f32[128,1024]{1,0:T(8,128)}, u32[]{:S(2)}) copy-start(f32[128,1024]{1,0:T(8,128)} %get-tuple-element.37.down_own_ref) | copy-start | bytes 1572868
  104.6 6.5 %collective-permute-start.6 = (bf16[64,1024]{1,0:T(8,128)(2,1)}, bf16[64,1024]{1,0:T(8,128)(2,1)S(1)}, u32[]{:S(2)}, u32[]{:S(2)}) collective-permute-start(bf16[64,1024]{1,0:T(8,128)(2,1)} %get-tuple-element.29), channel_id=1, source_target_pairs={{0,32},{32,64},{64,96},{96,128},{128,160},{160,192},{192,224},{224... | collective-permute-start | bytes 393224 | tf_op jit(solution)/shard_map/ppermute | solution.py:211
  106.1 5.2 %collective-permute-start.7 = (bf16[64,1024]{1,0:T(8,128)(2,1)}, bf16[64,1024]{1,0:T(8,128)(2,1)S(1)}, u32[]{:S(2)}, u32[]{:S(2)}) collective-permute-start(bf16[64,1024]{1,0:T(8,128)(2,1)} %get-tuple-element.30), channel_id=1, source_target_pairs={{0,224},{32,0},{64,32},{96,64},{128,96},{160,128},{192,160},{224,1... | collective-permute-start | bytes 393224 | tf_op jit(solution)/shard_map/ppermute | solution.py:211
  111.3 1.0 copy-start.6
  112.4 1.0 copy-start.7
  113.5 17.9 %copy-start.2 = (f32[128,1024]{1,0:T(8,128)S(1)}, f32[128,1024]{1,0:T(8,128)}, u32[]{:S(2)}) copy-start(f32[128,1024]{1,0:T(8,128)} %get-tuple-element.40.up_own_ref) | copy-start | bytes 1572868
  113.5 17.9 %copy-start.3 = (f32[128,1024]{1,0:T(8,128)S(1)}, f32[128,1024]{1,0:T(8,128)}, u32[]{:S(2)}) copy-start(f32[128,1024]{1,0:T(8,128)} %get-tuple-element.41.down_own_ref) | copy-start | bytes 1572868
  113.5 7.7 %collective-permute-start.8 = (bf16[128,1024]{1,0:T(8,128)(2,1)S(1)}, bf16[128,1024]{1,0:T(8,128)(2,1)S(1)}, u32[]{:S(2)}, u32[]{:S(2)}) collective-permute-start(bf16[128,1024]{1,0:T(8,128)(2,1)S(1)} %get-tuple-element.34), channel_id=1, source_target_pairs={{0,32},{32,64},{64,96},{96,128},{128,160},{160,192},{192,224},{224... | collective-permute-start | bytes 786440 | tf_op jit(solution)/shard_map/ppermute | solution.py:211
  115.0 6.5 %collective-permute-start.9 = (bf16[128,1024]{1,0:T(8,128)(2,1)S(1)}, bf16[128,1024]{1,0:T(8,128)(2,1)S(1)}, u32[]{:S(2)}, u32[]{:S(2)}) collective-permute-start(bf16[128,1024]{1,0:T(8,128)(2,1)S(1)} %get-tuple-element.35), channel_id=1, source_target_pairs={{0,224},{32,0},{64,32},{96,64},{128,96},{160,128},{192,160},{224,1... | collective-permute-start | bytes 786440 | tf_op jit(solution)/shard_map/ppermute | solution.py:211
  121.6 13.3 %copy-start = (f32[64,1024]{1,0:T(8,128)S(1)}, f32[64,1024]{1,0:T(8,128)}, u32[]{:S(2)}) copy-start(f32[64,1024]{1,0:T(8,128)} %multiply_cosine_fusion.wave_ref) | copy-start | bytes 786436
  121.6 13.3 %copy-start.8 = (s32[32]{0:T(128)S(1)}, s32[32]{0:T(128)}, u32[]{:S(2)}) copy-start(s32[32]{0:T(128)} %param.10) | copy-start | bytes 388
  121.6 7.7 %collective-permute-start.10 = (bf16[128,1024]{1,0:T(8,128)(2,1)S(1)}, bf16[128,1024]{1,0:T(8,128)(2,1)S(1)}, u32[]{:S(2)}, u32[]{:S(2)}) collective-permute-start(bf16[128,1024]{1,0:T(8,128)(2,1)S(1)} %get-tuple-element.38), channel_id=1, source_target_pairs={{0,32},{32,64},{64,96},{96,128},{128,160},{160,192},{192,224},{224... | collective-permute-start | bytes 786440 | tf_op jit(solution)/shard_map/ppermute | solution.py:211
  124.9 6.4 %collective-permute-start.11 = (bf16[128,1024]{1,0:T(8,128)(2,1)S(1)}, bf16[128,1024]{1,0:T(8,128)(2,1)S(1)}, u32[]{:S(2)}, u32[]{:S(2)}) collective-permute-start(bf16[128,1024]{1,0:T(8,128)(2,1)S(1)} %get-tuple-element.39), channel_id=1, source_target_pairs={{0,224},{32,0},{64,32},{96,64},{128,96},{160,128},{192,160},{224,1... | collective-permute-start | bytes 786440 | tf_op jit(solution)/shard_map/ppermute | solution.py:211
  131.5 9.5 %copy-start.1 = (f32[128,1024]{1,0:T(8,128)S(1)}, f32[128,1024]{1,0:T(8,128)}, u32[]{:S(2)}) copy-start(f32[128,1024]{1,0:T(8,128)} %get-tuple-element.28.own) | copy-start | bytes 1572868
  131.5 7.8 %collective-permute-start.12 = (bf16[128,1024]{1,0:T(8,128)(2,1)S(1)}, bf16[128,1024]{1,0:T(8,128)(2,1)S(1)}, u32[]{:S(2)}, u32[]{:S(2)}) collective-permute-start(bf16[128,1024]{1,0:T(8,128)(2,1)S(1)} %get-tuple-element.42), channel_id=1, source_target_pairs={{0,32},{32,64},{64,96},{96,128},{128,160},{160,192},{192,224},{224... | collective-permute-start | bytes 786440 | tf_op jit(solution)/shard_map/ppermute | solution.py:211
  134.6 6.4 %collective-permute-start.13 = (bf16[128,1024]{1,0:T(8,128)(2,1)S(1)}, bf16[128,1024]{1,0:T(8,128)(2,1)S(1)}, u32[]{:S(2)}, u32[]{:S(2)}) collective-permute-start(bf16[128,1024]{1,0:T(8,128)(2,1)S(1)} %get-tuple-element.43), channel_id=1, source_target_pairs={{0,224},{32,0},{64,32},{96,64},{128,96},{160,128},{192,160},{224,1... | collective-permute-start | bytes 786440 | tf_op jit(solution)/shard_map/ppermute | solution.py:211

commit v2 on v1

--- a/solution.py
+++ b/solution.py
@@ -228,6 +228,33 @@
     return pltpu.with_memory_space_constraint(x, pltpu.VMEM)
 
 
+def fetch_add_kernel(up_ref, down_ref, up_hbm, down_hbm, up_out, down_out, up_own, down_own, sems):
+    copies = [
+        pltpu.make_async_copy(up_hbm, up_own, sems.at[0]),
+        pltpu.make_async_copy(down_hbm, down_own, sems.at[1]),
+    ]
+    for copy in copies:
+        copy.start()
+    for copy in copies:
+        copy.wait()
+    add_kernel(up_ref, down_ref, up_own, down_own, up_out, down_out)
+
+
+def first_ring_add(up, down, up_own, down_own):
+    vmem = pl.BlockSpec(memory_space=pltpu.VMEM)
+    hbm = pl.BlockSpec(memory_space=pltpu.HBM)
+    result = pltpu.VMEM(up_own.shape, up.dtype)
+    own = pltpu.VMEM(up_own.shape, up_own.dtype)
+    return pl.pallas_call(
+        fetch_add_kernel,
+        out_shape=(result, result),
+        in_specs=[vmem, vmem, hbm, hbm],
+        out_specs=(vmem, vmem),
+        scratch_shapes=[own, own, pltpu.SemaphoreType.DMA((2,))],
+        name="ring_add_first",
+    )(in_vmem(up), in_vmem(down), up_own, down_own)
+
+
 def ring_add(*operands):
     vmem = pl.BlockSpec(memory_space=pltpu.VMEM)
     result = pltpu.VMEM(operands[2].shape, operands[0].dtype)
@@ -252,7 +279,8 @@
             own = chunks[distance]
             if distance == middle - 1:
                 own = after(own, token)
-            up, down = ring_add(up, down, own, chunks[size - distance])
+            add = first_ring_add if distance == middle - 1 else ring_add
+            up, down = add(up, down, own, chunks[size - distance])
     return chunks[0], up, down
 
 

time: 143 us -> 142 us (level)
  local copies, waits for them, and re-layouts: 4.06 us -> 1.98 us
    unnamed x24 -> x20, local copies, waits for them, and re-layouts: 2.13 us -> 0.05 us
where the time goes in v2:
time: 142 us; the launch traced here: 141 us
  starting transfers between devices  51.6 us (36%)
  Pallas kernels  47.6 us (34%)
  waiting for transfers between devices  36.7 us (26%)
  other arithmetic  2.32 us (2%)
  local copies, waits for them, and re-layouts  1.98 us (1%)
    pallas_call x4, Pallas kernels, sum_pieces(): pl.pallas_call(functools.partial(sums_kernel, len(pieces), int(base is no...  27.2 us
    ppermute x14, starting transfers between devices, shifted(): return lax.ppermute(x, axis, [(i, (i + by) % size) for i in range(size)])  20.1 us
    ppermute x14, waiting for transfers between devices, shifted(): return lax.ppermute(x, axis, [(i, (i + by) % size) for i in range(size)])  16.2 us
    all_to_all x1, starting transfers between devices, body(): arrived = lax.all_to_all(sums, BLK, split_axis=0, concat_axis=0, tiled=True)  12.5 us
    all_to_all x1, starting transfers between devices, body(): lax.all_to_all(summed, BLK, split_axis=0, concat_axis=0, tiled=True)  11.3 us
    all_to_all x1, waiting for transfers between devices, body(): arrived = lax.all_to_all(sums, BLK, split_axis=0, concat_axis=0, tiled=True)  9.13 us
    all_to_all x1, waiting for transfers between devices, body(): lax.all_to_all(pieces, 'lblk', split_axis=0, concat_axis=0, tiled=True)  6.02 us
    pallas_call x1, Pallas kernels, legendre_pair(): pl.pallas_call(legendre_kernel, out_shape=jax.ShapeDtypeStruct((blocks, 1...  5.41 us
  transfers between devices with their start and end apart: 18, of which 10 were waited for; matrix products, arithmetic and copies ran while one was open for 1% of the time, Pallas kernels for 30%

profile of v2, /device:TPU:8, one launch (start us, length us, event | category | flops | bytes accessed | tf_op | source)
XLA Modules:
  0.0 141.1 jit_solution(7631598120182130734)
XLA Ops:
  1.5 1.7 %multiply_cosine_fusion.wave_ref = f32[64,1024]{1,0:T(8,128)} fusion(s32[64]{0:T(128)S(1)} %iota.19, s32[64]{0:T(128)S(1)} %mul.32), kind=kLoop, calls=%fused_computation | loop fusion | flops 327680 | bytes 262656 | tf_op jit(solution)/shard_map/cos | solution.py:46
  3.2 3.0 %pack.1 = (bf16[528,1024]{1,0:T(8,128)(2,1)}, bf16[528,1024]{1,0:T(8,128)(2,1)}) custom-call(bf16[1024,1024]{1,0:T(8,128)(2,1)} %bitcast.16, s32[1,1024]{1,0:T(1,128)} %bitcast.20, s32[1,1024]{1,0:T(1,128)} %key_ref.3), custom_call_target="tpu_custom_call" | custom-call | tf_op jit(solution)/shard_map/pack/pallas_call | solution.py:312
  6.2 2.2 %collective-permute-start.2 = (bf16[528,1024]{1,0:T(8,128)(2,1)}, bf16[528,1024]{1,0:T(8,128)(2,1)S(1)}, u32[]{:S(2)}, u32[]{:S(2)}) collective-permute-start(bf16[528,1024]{1,0:T(8,128)(2,1)} %get-tuple-element.26.refs_1_.refs_3_), channel_id=1, source_target_pairs={{0,24},{8,0},{16,8},{24,16},{1,25},{9,1},{17,9},{25,17},{2,26},{10... | collective-permute-start | bytes 3244040 | tf_op jit(solution)/shard_map/ppermute | solution.py:211
  8.4 4.5 %modes.1 = f32[32,8,128]{2,1,0:T(8,128)} custom-call(bf16[1024,1024]{1,0:T(8,128)(2,1)} %bitcast.17, s32[1,1024]{1,0:T(1,128)} %bitcast.21, s32[1,1024]{1,0:T(1,128)} %key_ref.3, f32[64,1024]{1,0:T(8,128)} %multiply_cosine_fusion.wave_ref), custom_call_target="tpu_custom_call" | custom-call | tf_op jit(solution)/shard_map/modes/pallas_call | solution.py:91
  12.9 12.5 %all-to-all-start = ((f32[32,8,128]{2,1,0:T(8,128)}), f32[32,8,128]{2,1,0:T(8,128)S(1)}, u32[]{:S(2)}, u32[]{:S(2)}) async-start(f32[32,8,128]{2,1,0:T(8,128)} %modes.1), calls=%async_computation | async-start | bytes 262144 | tf_op jit(solution)/shard_map/all_to_all | solution.py:426
  25.4 1.5 %collective-permute-start.4 = (bf16[528,1024]{1,0:T(8,128)(2,1)}, bf16[528,1024]{1,0:T(8,128)(2,1)}, u32[]{:S(2)}, u32[]{:S(2)}) collective-permute-start(bf16[528,1024]{1,0:T(8,128)(2,1)} %get-tuple-element.26.refs_1_.refs_3_), channel_id=1, source_target_pairs={{0,8},{8,16},{16,24},{24,0},{1,9},{9,17},{17,25},{25,1},{2,10},{10... | collective-permute-start | bytes 3244040 | tf_op jit(solution)/shard_map/ppermute | solution.py:211
  27.5 9.1 %all-to-all-done.in_ref = f32[32,8,128]{2,1,0:T(8,128)S(1)} async-done(((f32[32,8,128]{2,1,0:T(8,128)}), f32[32,8,128]{2,1,0:T(8,128)S(1)}, u32[]{:S(2)}, u32[]{:S(2)}) %all-to-all-start) | async-done | bytes 131104 | tf_op jit(solution)/shard_map/all_to_all | solution.py:426
  36.7 2.6 %collective-permute-start.3 = (bf16[528,1024]{1,0:T(8,128)(2,1)S(1)}, bf16[528,1024]{1,0:T(8,128)(2,1)}, u32[]{:S(2)}, u32[]{:S(2)}) collective-permute-start(bf16[528,1024]{1,0:T(8,128)(2,1)S(1)} %collective-permute-done.2.refs_1_.refs_3_), channel_id=1, source_target_pairs={{0,24},{8,0},{16,8},{24,16},{1,25},{9,1},{17,9},{25,17},{2,26},{10... | collective-permute-start | bytes 3244040 | tf_op jit(solution)/shard_map/ppermute | solution.py:211
  40.0 4.3 %all-to-all-start.1 = ((bf16[8,8,128]{2,1,0:T(8,128)(2,1)}), bf16[8,8,128]{2,1,0:T(8,128)(2,1)S(1)}, u32[]{:S(2)}, u32[]{:S(2)}) async-start(bf16[8,8,128]{2,1,0:T(8,128)(2,1)} %harmonics.1), calls=%async_computation.1 | async-start | bytes 32768 | tf_op jit(solution)/shard_map/all_to_all | solution.py:429
  44.3 5.4 %all-to-all-done.1.modes_ref = bf16[8,8,128]{2,1,0:T(8,128)(2,1)S(1)} async-done(((bf16[8,8,128]{2,1,0:T(8,128)(2,1)}), bf16[8,8,128]{2,1,0:T(8,128)(2,1)S(1)}, u32[]{:S(2)}, u32[]{:S(2)}) %all-to-all-start.1) | async-done | bytes 16416 | tf_op jit(solution)/shard_map/all_to_all | solution.py:429
  49.7 5.4 %legendre.1 = f32[8,12,256]{2,1,0:T(8,128)} custom-call(s32[1]{0:T(128)} %bitcast.first_ref, bf16[8,8,128]{2,1,0:T(8,128)(2,1)S(1)} %all-to-all-done.1.modes_ref, bf16[1,512,2048]{2,1,0:T(8,128)(2,1)} %leg_ref.1, bf16[1,512,2048]{2,1,0:T(8,128)(2,1)} %even_hbm.1, bf16[1,512,2048]{2,1,0:T(8,128)(2,1)} %odd_hbm.1), custom_call_target="tpu_custom_call" | custom-call | tf_op jit(solution)/shard_map/legendre/pallas_call | solution.py:155
  55.1 3.4 %all-to-all-start.2 = ((f32[8,12,256]{2,1,0:T(8,128)}), f32[8,12,256]{2,1,0:T(8,128)S(1)}, u32[]{:S(2)}, u32[]{:S(2)}) async-start(f32[8,12,256]{2,1,0:T(8,128)} %legendre.1), calls=%async_computation.2 | async-start | bytes 262144 | tf_op jit(solution)/shard_map/all_to_all | solution.py:432
  58.5 6.0 %all-to-all-done.2 = f32[8,12,256]{2,1,0:T(8,128)S(1)} async-done(((f32[8,12,256]{2,1,0:T(8,128)}), f32[8,12,256]{2,1,0:T(8,128)S(1)}, u32[]{:S(2)}, u32[]{:S(2)}) %all-to-all-start.2) | async-done | bytes 98336 | tf_op jit(solution)/shard_map/all_to_all | solution.py:432
  65.5 11.3 %all-to-all-start.3 = ((bf16[32,1,96]{2,1,0:T(2,128)(2,1)}), bf16[32,1,96]{2,1,0:T(2,128)(2,1)S(1)}, u32[]{:S(2)}, u32[]{:S(2)}) async-start(bf16[32,1,96]{2,1,0:T(2,128)(2,1)} %copy.14), calls=%async_computation.3 | async-start | bytes 32768 | tf_op jit(solution)/shard_map/all_to_all | solution.py:435
  77.4 6.2 %shard_map.86.refs_4_ = f32[1024,1024]{1,0:T(8,128)} custom-call(s32[2]{0:T(128)} %pad_add_fusion.place_ref, bf16[528,1024]{1,0:T(8,128)(2,1)} %get-tuple-element.23.refs_0_.refs_2_, bf16[528,1024]{1,0:T(8,128)(2,1)} %get-tuple-element.26.refs_1_.refs_3_, bf16[528,1024]{1,0:T(8,128)(2,1)} %get-tuple-element.23.refs_0_.refs_2_, ...), custom_call_target="tpu_custom_call" | custom-call | tf_op jit(solution)/shard_map/pallas_call | solution.py:358
  83.6 7.2 %shard_map.87.refs_4_ = f32[1024,1024]{1,0:T(8,128)} custom-call(s32[2]{0:T(128)} %pad_add_fusion.place_ref, bf16[528,1024]{1,0:T(8,128)(2,1)} %copy-done.8, bf16[528,1024]{1,0:T(8,128)(2,1)} %copy-done.7, bf16[528,1024]{1,0:T(8,128)(2,1)} %copy-done.8, bf16[528,1024]{1,0:T(8,128)(2,1)} %copy-done.7, f32[1024,1024]{1,0:T(8,128)} %shard_map.86.refs_4_), custom_call_target="tpu_custom_call" | custom-call | tf_op jit(solution)/shard_map/pallas_call | solution.py:358
  90.8 7.1 %shard_map.88.refs_4_ = f32[1024,1024]{1,0:T(8,128)} custom-call(s32[2]{0:T(128)} %pad_add_fusion.place_ref, bf16[528,1024]{1,0:T(8,128)(2,1)} %collective-permute-done.4.refs_0_.refs_2_, bf16[528,1024]{1,0:T(8,128)(2,1)} %collective-permute-done.5.refs_1_.refs_3_, bf16[528,1024]{1,0:T(8,128)(2,1)} %collective-permute-done.4.refs_0_.refs_2_, ...), custom_call_target="tpu_custom_call" | custom-call | tf_op jit(solution)/shard_map/pallas_call | solution.py:358
  97.9 6.7 %shard_map.89 = (f32[128,1024]{1,0:T(8,128)}, f32[128,1024]{1,0:T(8,128)}, f32[128,1024]{1,0:T(8,128)}, f32[128,1024]{1,0:T(8,128)}, bf16[64,1024]{1,0:T(8,128)(...) custom-call(s32[2]{0:T(128)} %pad_add_fusion.place_ref, ...), custom_call_target="tpu_custom_call" | custom-call | tf_op jit(solution)/shard_map/pallas_call | solution.py:358
  104.7 1.5 %collective-permute-start.6 = (bf16[64,1024]{1,0:T(8,128)(2,1)}, bf16[64,1024]{1,0:T(8,128)(2,1)S(1)}, u32[]{:S(2)}, u32[]{:S(2)}) collective-permute-start(bf16[64,1024]{1,0:T(8,128)(2,1)} %get-tuple-element.29), channel_id=1, source_target_pairs={{0,32},{32,64},{64,96},{96,128},{128,160},{160,192},{192,224},{224... | collective-permute-start | bytes 393224 | tf_op jit(solution)/shard_map/ppermute | solution.py:211
  106.2 1.8 %collective-permute-start.7 = (bf16[64,1024]{1,0:T(8,128)(2,1)}, bf16[64,1024]{1,0:T(8,128)(2,1)S(1)}, u32[]{:S(2)}, u32[]{:S(2)}) collective-permute-start(bf16[64,1024]{1,0:T(8,128)(2,1)} %get-tuple-element.30), channel_id=1, source_target_pairs={{0,224},{32,0},{64,32},{96,64},{128,96},{160,128},{192,160},{224,1... | collective-permute-start | bytes 393224 | tf_op jit(solution)/shard_map/ppermute | solution.py:211
  108.0 3.1 %collective-permute-done.6.up_ref = bf16[64,1024]{1,0:T(8,128)(2,1)S(1)} collective-permute-done((bf16[64,1024]{1,0:T(8,128)(2,1)}, bf16[64,1024]{1,0:T(8,128)(2,1)S(1)}, u32[]{:S(2)}, u32[]{:S(2)}) %collective-permute-start.6) | collective-permute-done | bytes 131104 | tf_op jit(solution)/shard_map/ppermute | solution.py:211
  111.4 1.3 ring_add_first.1
  112.7 1.5 %collective-permute-start.8 = (bf16[128,1024]{1,0:T(8,128)(2,1)S(1)}, bf16[128,1024]{1,0:T(8,128)(2,1)S(1)}, u32[]{:S(2)}, u32[]{:S(2)}) collective-permute-start(bf16[128,1024]{1,0:T(8,128)(2,1)S(1)} %get-tuple-element.34), channel_id=1, source_target_pairs={{0,32},{32,64},{64,96},{96,128},{128,160},{160,192},{192,224},{224... | collective-permute-start | bytes 786440 | tf_op jit(solution)/shard_map/ppermute | solution.py:211
  114.2 1.8 %collective-permute-start.9 = (bf16[128,1024]{1,0:T(8,128)(2,1)S(1)}, bf16[128,1024]{1,0:T(8,128)(2,1)S(1)}, u32[]{:S(2)}, u32[]{:S(2)}) collective-permute-start(bf16[128,1024]{1,0:T(8,128)(2,1)S(1)} %get-tuple-element.35), channel_id=1, source_target_pairs={{0,224},{32,0},{64,32},{96,64},{128,96},{160,128},{192,160},{224,1... | collective-permute-start | bytes 786440 | tf_op jit(solution)/shard_map/ppermute | solution.py:211
  116.0 4.3 %collective-permute-done.8.up_ref = bf16[128,1024]{1,0:T(8,128)(2,1)S(1)} collective-permute-done((bf16[128,1024]{1,0:T(8,128)(2,1)S(1)}, bf16[128,1024]{1,0:T(8,128)(2,1)S(1)}, u32[]{:S(2)}, u32[]{:S(2)}) %collective-permute-start.8) | collective-permute-done | bytes 262176 | tf_op jit(solution)/shard_map/ppermute | solution.py:211
  120.8 3.3 %collective-permute-start.10 = (bf16[128,1024]{1,0:T(8,128)(2,1)S(1)}, bf16[128,1024]{1,0:T(8,128)(2,1)S(1)}, u32[]{:S(2)}, u32[]{:S(2)}) collective-permute-start(bf16[128,1024]{1,0:T(8,128)(2,1)S(1)} %get-tuple-element.38), channel_id=1, source_target_pairs={{0,32},{32,64},{64,96},{96,128},{128,160},{160,192},{192,224},{224... | collective-permute-start | bytes 786440 | tf_op jit(solution)/shard_map/ppermute | solution.py:211
  124.1 4.3 %collective-permute-done.10.up_ref = bf16[128,1024]{1,0:T(8,128)(2,1)S(1)} collective-permute-done((bf16[128,1024]{1,0:T(8,128)(2,1)S(1)}, bf16[128,1024]{1,0:T(8,128)(2,1)S(1)}, u32[]{:S(2)}, u32[]{:S(2)}) %collective-permute-start.10) | collective-permute-done | bytes 262176 | tf_op jit(solution)/shard_map/ppermute | solution.py:211
  128.5 2.1 %collective-permute-done.11.down_ref = bf16[128,1024]{1,0:T(8,128)(2,1)S(1)} collective-permute-done((bf16[128,1024]{1,0:T(8,128)(2,1)S(1)}, bf16[128,1024]{1,0:T(8,128)(2,1)S(1)}, u32[]{:S(2)}, u32[]{:S(2)}) %collective-permute-start.11) | collective-permute-done | bytes 262176 | tf_op jit(solution)/shard_map/ppermute | solution.py:211
  130.7 3.1 %collective-permute-start.12 = (bf16[128,1024]{1,0:T(8,128)(2,1)S(1)}, bf16[128,1024]{1,0:T(8,128)(2,1)S(1)}, u32[]{:S(2)}, u32[]{:S(2)}) collective-permute-start(bf16[128,1024]{1,0:T(8,128)(2,1)S(1)} %get-tuple-element.42), channel_id=1, source_target_pairs={{0,32},{32,64},{64,96},{96,128},{128,160},{160,192},{192,224},{224... | collective-permute-start | bytes 786440 | tf_op jit(solution)/shard_map/ppermute | solution.py:211
  134.1 4.4 %fields.1 = f32[2,2,1,8,8192]{4,3,2,1,0:T(8,128)} custom-call(f32[12,8,32]{2,1,0:T(8,128)S(1)} %bitcast.14, s32[1,32]{1,0:T(1,128)S(1)} %bitcast.15, f32[64,1024]{1,0:T(8,128)S(1)} %copy-done), custom_call_target="tpu_custom_call" | custom-call | tf_op jit(solution)/shard_map/fields/pallas_call | solution.py:198
  138.6 1.7 %collective-permute-done.13.down = bf16[128,1024]{1,0:T(8,128)(2,1)S(1)} collective-permute-done((bf16[128,1024]{1,0:T(8,128)(2,1)S(1)}, bf16[128,1024]{1,0:T(8,128)(2,1)S(1)}, u32[]{:S(2)}, u32[]{:S(2)}) %collective-permute-start.13) | collective-permute-done | bytes 262176 | tf_op jit(solution)/shard_map/ppermute | solution.py:211
  140.2 0.9 maps.1
  (50 shorter events, 4.9 us)
Async XLA Ops:
  6.2 30.4 %collective-permute-start.2 = (bf16[528,1024]{1,0:T(8,128)(2,1)}, bf16[528,1024]{1,0:T(8,128)(2,1)S(1)}, u32[]{:S(2)}, u32[]{:S(2)}) collective-permute-start(bf16[528,1024]{1,0:T(8,128)(2,1)} %get-tuple-element.26.refs_1_.refs_3_), channel_id=1, source_target_pairs={{0,24},{8,0},{16,8},{24,16},{1,25},{9,1},{17,9},{25,17},{2,26},{10... | collective-permute-start | bytes 3244040 | tf_op jit(solution)/shard_map/ppermute | solution.py:211
  8.4 18.6 %copy-start.9 = (bf16[528,1024]{1,0:T(8,128)(2,1)S(1)}, bf16[528,1024]{1,0:T(8,128)(2,1)}, u32[]{:S(2)}) copy-start(bf16[528,1024]{1,0:T(8,128)(2,1)} %get-tuple-element.23.refs_0_.refs_2_) | copy-start | bytes 3244036
  8.4 30.9 %collective-permute-start = (bf16[528,1024]{1,0:T(8,128)(2,1)}, bf16[528,1024]{1,0:T(8,128)(2,1)S(1)}, u32[]{:S(2)}, u32[]{:S(2)}) collective-permute-start(bf16[528,1024]{1,0:T(8,128)(2,1)} %get-tuple-element.23.refs_0_.refs_2_), channel_id=1, source_target_pairs={{0,8},{8,16},{16,24},{24,0},{1,9},{9,17},{17,25},{25,1},{2,10},{10... | collective-permute-start | bytes 3244040 | tf_op jit(solution)/shard_map/ppermute | solution.py:211
  12.9 23.8 %all-to-all-start = ((f32[32,8,128]{2,1,0:T(8,128)}), f32[32,8,128]{2,1,0:T(8,128)S(1)}, u32[]{:S(2)}, u32[]{:S(2)}) async-start(f32[32,8,128]{2,1,0:T(8,128)} %modes.1), calls=%async_computation | async-start | bytes 262144 | tf_op jit(solution)/shard_map/all_to_all | solution.py:426
  25.4 65.4 %collective-permute-start.4 = (bf16[528,1024]{1,0:T(8,128)(2,1)}, bf16[528,1024]{1,0:T(8,128)(2,1)}, u32[]{:S(2)}, u32[]{:S(2)}) collective-permute-start(bf16[528,1024]{1,0:T(8,128)(2,1)} %get-tuple-element.26.refs_1_.refs_3_), channel_id=1, source_target_pairs={{0,8},{8,16},{16,24},{24,0},{1,9},{9,17},{17,25},{25,1},{2,10},{10... | collective-permute-start | bytes 3244040 | tf_op jit(solution)/shard_map/ppermute | solution.py:211
  27.0 63.8 %collective-permute-start.5 = (bf16[528,1024]{1,0:T(8,128)(2,1)S(1)}, bf16[528,1024]{1,0:T(8,128)(2,1)}, u32[]{:S(2)}, u32[]{:S(2)}) collective-permute-start(bf16[528,1024]{1,0:T(8,128)(2,1)S(1)} %copy-done.9), channel_id=1, source_target_pairs={{0,24},{8,0},{16,8},{24,16},{1,25},{9,1},{17,9},{25,17},{2,26},{10... | collective-permute-start | bytes 3244040 | tf_op jit(solution)/shard_map/ppermute | solution.py:211
  36.7 18.4 %copy-start.7 = (bf16[528,1024]{1,0:T(8,128)(2,1)}, bf16[528,1024]{1,0:T(8,128)(2,1)S(1)}, u32[]{:S(2)}) copy-start(bf16[528,1024]{1,0:T(8,128)(2,1)S(1)} %collective-permute-done.2.refs_1_.refs_3_) | copy-start | bytes 3244036
  36.7 61.3 %collective-permute-start.3 = (bf16[528,1024]{1,0:T(8,128)(2,1)S(1)}, bf16[528,1024]{1,0:T(8,128)(2,1)}, u32[]{:S(2)}, u32[]{:S(2)}) collective-permute-start(bf16[528,1024]{1,0:T(8,128)(2,1)S(1)} %collective-permute-done.2.refs_1_.refs_3_), channel_id=1, source_target_pairs={{0,24},{8,0},{16,8},{24,16},{1,25},{9,1},{17,9},{25,17},{2,26},{10... | collective-permute-start | bytes 3244040 | tf_op jit(solution)/shard_map/ppermute | solution.py:211
  39.3 15.8 %copy-start.8 = (bf16[528,1024]{1,0:T(8,128)(2,1)}, bf16[528,1024]{1,0:T(8,128)(2,1)S(1)}, u32[]{:S(2)}) copy-start(bf16[528,1024]{1,0:T(8,128)(2,1)S(1)} %collective-permute-done.refs_0_.refs_2_) | copy-start | bytes 3244036
  39.3 58.7 %collective-permute-start.1 = (bf16[528,1024]{1,0:T(8,128)(2,1)S(1)}, bf16[528,1024]{1,0:T(8,128)(2,1)}, u32[]{:S(2)}, u32[]{:S(2)}) collective-permute-start(bf16[528,1024]{1,0:T(8,128)(2,1)S(1)} %collective-permute-done.refs_0_.refs_2_), channel_id=1, source_target_pairs={{0,8},{8,16},{16,24},{24,0},{1,9},{9,17},{17,25},{25,1},{2,10},{10... | collective-permute-start | bytes 3244040 | tf_op jit(solution)/shard_map/ppermute | solution.py:211
  40.0 9.7 %all-to-all-start.1 = ((bf16[8,8,128]{2,1,0:T(8,128)(2,1)}), bf16[8,8,128]{2,1,0:T(8,128)(2,1)S(1)}, u32[]{:S(2)}, u32[]{:S(2)}) async-start(bf16[8,8,128]{2,1,0:T(8,128)(2,1)} %harmonics.1), calls=%async_computation.1 | async-start | bytes 32768 | tf_op jit(solution)/shard_map/all_to_all | solution.py:429
  55.1 9.4 %all-to-all-start.2 = ((f32[8,12,256]{2,1,0:T(8,128)}), f32[8,12,256]{2,1,0:T(8,128)S(1)}, u32[]{:S(2)}, u32[]{:S(2)}) async-start(f32[8,12,256]{2,1,0:T(8,128)} %legendre.1), calls=%async_computation.2 | async-start | bytes 262144 | tf_op jit(solution)/shard_map/all_to_all | solution.py:432
  65.5 42.5 %all-to-all-start.3 = ((bf16[32,1,96]{2,1,0:T(2,128)(2,1)}), bf16[32,1,96]{2,1,0:T(2,128)(2,1)S(1)}, u32[]{:S(2)}, u32[]{:S(2)}) async-start(bf16[32,1,96]{2,1,0:T(2,128)(2,1)} %copy.14), calls=%async_computation.3 | async-start | bytes 32768 | tf_op jit(solution)/shard_map/all_to_all | solution.py:435
  104.7 16.1 %copy-start.4 = (f32[128,1024]{1,0:T(8,128)S(1)}, f32[128,1024]{1,0:T(8,128)}, u32[]{:S(2)}) copy-start(f32[128,1024]{1,0:T(8,128)} %get-tuple-element.36.up_own_ref) | copy-start | bytes 1572868
  104.7 16.1 %copy-start.5 = (f32[128,1024]{1,0:T(8,128)S(1)}, f32[128,1024]{1,0:T(8,128)}, u32[]{:S(2)}) copy-start(f32[128,1024]{1,0:T(8,128)} %get-tuple-element.37.down_own_ref) | copy-start | bytes 1572868
  104.7 6.5 %collective-permute-start.6 = (bf16[64,1024]{1,0:T(8,128)(2,1)}, bf16[64,1024]{1,0:T(8,128)(2,1)S(1)}, u32[]{:S(2)}, u32[]{:S(2)}) collective-permute-start(bf16[64,1024]{1,0:T(8,128)(2,1)} %get-tuple-element.29), channel_id=1, source_target_pairs={{0,32},{32,64},{64,96},{96,128},{128,160},{160,192},{192,224},{224... | collective-permute-start | bytes 393224 | tf_op jit(solution)/shard_map/ppermute | solution.py:211
  106.2 5.2 %collective-permute-start.7 = (bf16[64,1024]{1,0:T(8,128)(2,1)}, bf16[64,1024]{1,0:T(8,128)(2,1)S(1)}, u32[]{:S(2)}, u32[]{:S(2)}) collective-permute-start(bf16[64,1024]{1,0:T(8,128)(2,1)} %get-tuple-element.30), channel_id=1, source_target_pairs={{0,224},{32,0},{64,32},{96,64},{128,96},{160,128},{192,160},{224,1... | collective-permute-start | bytes 393224 | tf_op jit(solution)/shard_map/ppermute | solution.py:211
  112.7 17.9 %copy-start.2 = (f32[128,1024]{1,0:T(8,128)S(1)}, f32[128,1024]{1,0:T(8,128)}, u32[]{:S(2)}) copy-start(f32[128,1024]{1,0:T(8,128)} %get-tuple-element.40.up_own_ref) | copy-start | bytes 1572868
  112.7 17.9 %copy-start.3 = (f32[128,1024]{1,0:T(8,128)S(1)}, f32[128,1024]{1,0:T(8,128)}, u32[]{:S(2)}) copy-start(f32[128,1024]{1,0:T(8,128)} %get-tuple-element.41.down_own_ref) | copy-start | bytes 1572868
  112.7 7.7 %collective-permute-start.8 = (bf16[128,1024]{1,0:T(8,128)(2,1)S(1)}, bf16[128,1024]{1,0:T(8,128)(2,1)S(1)}, u32[]{:S(2)}, u32[]{:S(2)}) collective-permute-start(bf16[128,1024]{1,0:T(8,128)(2,1)S(1)} %get-tuple-element.34), channel_id=1, source_target_pairs={{0,32},{32,64},{64,96},{96,128},{128,160},{160,192},{192,224},{224... | collective-permute-start | bytes 786440 | tf_op jit(solution)/shard_map/ppermute | solution.py:211
  114.2 6.5 %collective-permute-start.9 = (bf16[128,1024]{1,0:T(8,128)(2,1)S(1)}, bf16[128,1024]{1,0:T(8,128)(2,1)S(1)}, u32[]{:S(2)}, u32[]{:S(2)}) collective-permute-start(bf16[128,1024]{1,0:T(8,128)(2,1)S(1)} %get-tuple-element.35), channel_id=1, source_target_pairs={{0,224},{32,0},{64,32},{96,64},{128,96},{160,128},{192,160},{224,1... | collective-permute-start | bytes 786440 | tf_op jit(solution)/shard_map/ppermute | solution.py:211
  120.8 13.3 %copy-start = (f32[64,1024]{1,0:T(8,128)S(1)}, f32[64,1024]{1,0:T(8,128)}, u32[]{:S(2)}) copy-start(f32[64,1024]{1,0:T(8,128)} %multiply_cosine_fusion.wave_ref) | copy-start | bytes 786436
  120.8 13.3 %copy-start.6 = (s32[32]{0:T(128)S(1)}, s32[32]{0:T(128)}, u32[]{:S(2)}) copy-start(s32[32]{0:T(128)} %param.10) | copy-start | bytes 388
  120.8 7.7 %collective-permute-start.10 = (bf16[128,1024]{1,0:T(8,128)(2,1)S(1)}, bf16[128,1024]{1,0:T(8,128)(2,1)S(1)}, u32[]{:S(2)}, u32[]{:S(2)}) collective-permute-start(bf16[128,1024]{1,0:T(8,128)(2,1)S(1)} %get-tuple-element.38), channel_id=1, source_target_pairs={{0,32},{32,64},{64,96},{96,128},{128,160},{160,192},{192,224},{224... | collective-permute-start | bytes 786440 | tf_op jit(solution)/shard_map/ppermute | solution.py:211
  124.1 6.4 %collective-permute-start.11 = (bf16[128,1024]{1,0:T(8,128)(2,1)S(1)}, bf16[128,1024]{1,0:T(8,128)(2,1)S(1)}, u32[]{:S(2)}, u32[]{:S(2)}) collective-permute-start(bf16[128,1024]{1,0:T(8,128)(2,1)S(1)} %get-tuple-element.39), channel_id=1, source_target_pairs={{0,224},{32,0},{64,32},{96,64},{128,96},{160,128},{192,160},{224,1... | collective-permute-start | bytes 786440 | tf_op jit(solution)/shard_map/ppermute | solution.py:211
  130.7 9.5 %copy-start.1 = (f32[128,1024]{1,0:T(8,128)S(1)}, f32[128,1024]{1,0:T(8,128)}, u32[]{:S(2)}) copy-start(f32[128,1024]{1,0:T(8,128)} %get-tuple-element.28.own) | copy-start | bytes 1572868
  130.7 7.8 %collective-permute-start.12 = (bf16[128,1024]{1,0:T(8,128)(2,1)S(1)}, bf16[128,1024]{1,0:T(8,128)(2,1)S(1)}, u32[]{:S(2)}, u32[]{:S(2)}) collective-permute-start(bf16[128,1024]{1,0:T(8,128)(2,1)S(1)} %get-tuple-element.42), channel_id=1, source_target_pairs={{0,32},{32,64},{64,96},{96,128},{128,160},{160,192},{192,224},{224... | collective-permute-start | bytes 786440 | tf_op jit(solution)/shard_map/ppermute | solution.py:211
  133.8 6.4 %collective-permute-start.13 = (bf16[128,1024]{1,0:T(8,128)(2,1)S(1)}, bf16[128,1024]{1,0:T(8,128)(2,1)S(1)}, u32[]{:S(2)}, u32[]{:S(2)}) collective-permute-start(bf16[128,1024]{1,0:T(8,128)(2,1)S(1)} %get-tuple-element.43), channel_id=1, source_target_pairs={{0,224},{32,0},{64,32},{96,64},{128,96},{160,128},{192,160},{224,1... | collective-permute-start | bytes 786440 | tf_op jit(solution)/shard_map/ppermute | solution.py:211
